TPU v7x, 256 devices: a whole 4x4x8 slice. The times are simulated.
256 devices in a mesh: row: 16 (over y, z_lo), col: 16 (over z_hi, x, core).
Axes of the slice: x: 4, y: 4, z: 8 (z_hi: 2, z_lo: 4; z = z_hi * 4 + z_lo), core: 2. Of those that a mesh axis runs over, the one named last changes fastest.
Arguments:
- start_vectors: float32 [64, 32768], P(None, ('row', 'col')), may hold values from -6 to 6
- cluster_order: int32 [256, 128], P(('row', 'col')), may hold values from 0 to 127, each once within a row
- weights: bfloat16 [32768, 16, 2048], P('row', 'col'), may hold values from 0 to 1, as said below
- block_mask: int32 [256, 16, 16], P('row', 'col'), may hold values 0 or 1
Outputs:
- embedding: float32 [64, 32768], P(None, ('row', 'col'))
Inputs may be any that keep to these rules, and one draw needn't show every extreme that they name: Each row of cluster_order holds every number of 0 to 127 once. `block_mask`: entries below the diagonal blocks are read only through their mirror. `weights`: every node except the last of its cluster block has a positive weight to the next node of its cluster block.
All inputs are finite; a program needn't handle non-finite values.
Results may differ from a plain program's by a relative error of at most 0.00087.
Values may be sent and summed in bfloat16 or wider, within the bound.
A program may use at most 64 MiB of HBM per device.

v0:
```python
import math

import jax
import jax.numpy as jnp
from jax import lax
from jax.sharding import PartitionSpec as P

ITERS = 3


def orthonormalize(panel_in):
    partial_gram = lax.dot_general(
        panel_in,
        panel_in,
        (((1,), (1,)), ((), ())),
        precision=lax.Precision.HIGHEST,
        preferred_element_type=jnp.float32,
    )
    total_gram = lax.psum(partial_gram, ("row", "col"))
    factor = jnp.linalg.cholesky(total_gram)
    return jax.scipy.linalg.solve_triangular(factor, panel_in, lower=True)


def collect_direct(term):
    return lax.psum_scatter(term, "col", scatter_dimension=1, tiled=True)


def direct_part(matrix, vectors):
    return lax.dot_general(
        lax.all_gather(vectors, "row", axis=1, tiled=True),
        matrix,
        (((1,), (1,)), ((), ())),
        preferred_element_type=jnp.float32,
    )


def local(start_vectors, cluster_order, weights, block_mask):
    row_index = lax.axis_index("row")
    col_index = lax.axis_index("col")
    row_count = lax.axis_size("row")
    col_count = lax.axis_size("col")
    block_len = start_vectors.shape[1]
    stored = weights[:, 0, :]
    live_mask = block_mask[:, 0, :]
    local_rows = row_index * col_count * block_len + jnp.arange(
        col_count * block_len, dtype=jnp.int32
    )
    col_position = jnp.arange(row_count * block_len, dtype=jnp.int32)
    local_cols = (
        col_position // block_len * col_count + col_index
    ) * block_len + col_position % block_len
    row_spans = row_index * col_count + jnp.arange(col_count, dtype=jnp.int32)
    col_spans = jnp.arange(row_count, dtype=jnp.int32) * col_count + col_index
    same_block = row_spans[:, None] == col_spans[None, :]
    keep_upper = ((live_mask > 0) | same_block)[:, None, :, None] & (
        local_rows.reshape(col_count, block_len, 1, 1)
        < local_cols.reshape(1, 1, row_count, block_len)
    )
    zero_value = jnp.zeros((), jnp.bfloat16)
    upper_part = jnp.where(
        keep_upper, stored.reshape(col_count, block_len, row_count, block_len), zero_value
    )
    ones_cols = jnp.ones((row_count * block_len,), jnp.bfloat16)
    matrix = upper_part.reshape(col_count * block_len, row_count * block_len)
    ones_rows = jnp.ones((col_count * block_len,), jnp.bfloat16)

    def mirror_sums(term):
        return lax.psum_scatter(term, "row", scatter_dimension=1, tiled=True)

    row_totals = jnp.dot(matrix, ones_cols, preferred_element_type=jnp.float32)[None, :]
    col_totals = jnp.dot(ones_rows, matrix, preferred_element_type=jnp.float32)[None, :]
    degree = collect_direct(row_totals) + mirror_sums(col_totals)
    inverse_root = 1.0 / jnp.sqrt(degree)
    picked = jnp.take_along_axis(
        start_vectors, jnp.broadcast_to(cluster_order, start_vectors.shape), axis=1
    )
    panel_now = orthonormalize(picked)
    for round_index in range(ITERS):
        vectors = (inverse_root * panel_now).astype(jnp.bfloat16)
        panel_now = orthonormalize(
            panel_now
            + inverse_root
            * (
                collect_direct(direct_part(matrix, vectors))
                + mirror_sums(
                    jnp.dot(
                        lax.all_gather(vectors, "col", axis=1, tiled=True),
                        matrix,
                        preferred_element_type=jnp.float32,
                    )
                )
            )
        )
    total_nodes = block_len * row_count * col_count
    return math.sqrt(total_nodes) * panel_now


def solution(mesh):
    placed = (
        P(None, ("row", "col")),
        P(("row", "col"), None),
        P("row", "col", None),
        P("row", "col", None),
    )
    return jax.shard_map(
        local, mesh=mesh, in_specs=placed, out_specs=P(None, ("row", "col")), check_vma=False
    )
```

profile of v0, /device:TPU:1, one launch (start us, length us, event | category | flops | bytes accessed | tf_op | source)
XLA Modules:
  0.0 1080.2 jit_solution(14854760492870772984)
XLA Ops:
  8.5 7.7 fusion
  23.0 7.7 convolution_bitcast_fusion
  30.9 50.7 %gather_fusion = f32[8192]{0:T(1024)S(1)} fusion(f32[64,128]{1,0:T(8,128)S(1)} %copy-done, s32[8192]{0:T(1024)S(1)} %or_bitcast_fusion), kind=kCustom, calls=%fused_computation | custom fusion | bytes 131072 | tf_op jit(solution)/shard_map/jit(take_along_axis)/gather | solution.py:74
  81.7 82.8 %psum.28 = f32[64,64]{0,1:T(8,128)S(1)} all-reduce(f32[64,64]{0,1:T(8,128)S(1)} %fusion.16), channel_id=1, replica_groups=mesh['row'=16,'col'=16] {'row','col'}, use_global_device_ids=true, to_apply=%region_0.1 | all-reduce | flops 4096 | bytes 32768 | tf_op jit(solution)/shard_map/psum | solution.py:19
  183.7 32.5 %all_gather.18 = bf16[64,2048]{1,0:T(8,128)(2,1)S(1)} all-gather(bf16[64,128]{1,0:T(8,128)(2,1)S(1)} %get-tuple-element.6), channel_id=1, replica_groups=mesh['row'=16,'col'=16] {'row'}, dimensions={1}, use_global_device_ids=true | all-gather | bytes 278528 | tf_op jit(solution)/shard_map/all_gather | solution.py:30
  216.2 6.9 fusion.59
  223.1 50.3 %all_gather.19 = bf16[64,2048]{1,0:T(8,128)(2,1)S(1)} all-gather(bf16[64,128]{1,0:T(8,128)(2,1)S(1)} %get-tuple-element.6), channel_id=1, replica_groups=mesh['row'=16,'col'=16] {'col'}, dimensions={1}, use_global_device_ids=true | all-gather | bytes 278528 | tf_op jit(solution)/shard_map/all_gather | solution.py:87
  279.4 35.2 %reduce-scatter.13.cloned.1.call-done = f32[64,128]{1,0:T(8,128)} async-done(((f32[64,2048]{1,0:T(8,128)}), f32[64,128]{1,0:T(8,128)}) %reduce-scatter.13.cloned.1.call-update) | async-done | bytes 32784 | tf_op jit(solution)/shard_map/reduce_scatter | solution.py:25
  314.6 75.0 %reduce-scatter.15.cloned.1.call-done = f32[64,128]{1,0:T(8,128)} async-done(((f32[64,2048]{1,0:T(8,128)}), f32[64,128]{1,0:T(8,128)}) %reduce-scatter.15.cloned.1.call-update) | async-done | bytes 32784 | tf_op jit(solution)/shard_map/reduce_scatter | solution.py:68
  390.6 85.2 %psum.29 = f32[64,64]{0,1:T(8,128)S(1)} all-reduce(f32[64,64]{0,1:T(8,128)S(1)} %fusion.61), channel_id=1, replica_groups=mesh['row'=16,'col'=16] {'row','col'}, use_global_device_ids=true, to_apply=%region_7.10 | all-reduce | flops 4096 | bytes 32768 | tf_op jit(solution)/shard_map/psum | solution.py:19
  475.8 5.8 cholesky.85
  488.2 34.1 %all_gather.20 = bf16[64,2048]{1,0:T(8,128)(2,1)S(1)} all-gather(bf16[64,128]{1,0:T(8,128)(2,1)S(1)} %get-tuple-element.9), channel_id=1, replica_groups=mesh['row'=16,'col'=16] {'row'}, dimensions={1}, use_global_device_ids=true | all-gather | bytes 278528 | tf_op jit(solution)/shard_map/all_gather | solution.py:30
  522.3 6.9 fusion.62
  529.2 36.1 %all_gather.21 = bf16[64,2048]{1,0:T(8,128)(2,1)S(1)} all-gather(bf16[64,128]{1,0:T(8,128)(2,1)S(1)} %get-tuple-element.9), channel_id=1, replica_groups=mesh['row'=16,'col'=16] {'col'}, dimensions={1}, use_global_device_ids=true | all-gather | bytes 278528 | tf_op jit(solution)/shard_map/all_gather | solution.py:87
  571.2 35.5 %reduce-scatter.17.cloned.1.call-done = f32[64,128]{1,0:T(8,128)} async-done(((f32[64,2048]{1,0:T(8,128)}), f32[64,128]{1,0:T(8,128)}) %reduce-scatter.17.cloned.1.call-update) | async-done | bytes 32784 | tf_op jit(solution)/shard_map/reduce_scatter | solution.py:25
  606.7 74.7 %reduce-scatter.19.cloned.1.call-done = f32[64,128]{1,0:T(8,128)} async-done(((f32[64,2048]{1,0:T(8,128)}), f32[64,128]{1,0:T(8,128)}) %reduce-scatter.19.cloned.1.call-update) | async-done | bytes 32784 | tf_op jit(solution)/shard_map/reduce_scatter | solution.py:68
  682.4 85.6 %psum.30 = f32[64,64]{0,1:T(8,128)S(1)} all-reduce(f32[64,64]{0,1:T(8,128)S(1)} %fusion.64), channel_id=1, replica_groups=mesh['row'=16,'col'=16] {'row','col'}, use_global_device_ids=true, to_apply=%region_10.13 | all-reduce | flops 4096 | bytes 32768 | tf_op jit(solution)/shard_map/psum | solution.py:19
  768.1 5.8 cholesky.96
  780.4 34.1 %all_gather.22 = bf16[64,2048]{1,0:T(8,128)(2,1)S(1)} all-gather(bf16[64,128]{1,0:T(8,128)(2,1)S(1)} %get-tuple-element.11), channel_id=1, replica_groups=mesh['row'=16,'col'=16] {'row'}, dimensions={1}, use_global_device_ids=true | all-gather | bytes 278528 | tf_op jit(solution)/shard_map/all_gather | solution.py:30
  814.5 6.9 fusion.65
  821.5 35.9 %all_gather.23 = bf16[64,2048]{1,0:T(8,128)(2,1)S(1)} all-gather(bf16[64,128]{1,0:T(8,128)(2,1)S(1)} %get-tuple-element.11), channel_id=1, replica_groups=mesh['row'=16,'col'=16] {'col'}, dimensions={1}, use_global_device_ids=true | all-gather | bytes 278528 | tf_op jit(solution)/shard_map/all_gather | solution.py:87
  863.2 35.7 %reduce-scatter.21.cloned.1.call-done = f32[64,128]{1,0:T(8,128)} async-done(((f32[64,2048]{1,0:T(8,128)}), f32[64,128]{1,0:T(8,128)}) %reduce-scatter.21.cloned.1.call-update) | async-done | bytes 32784 | tf_op jit(solution)/shard_map/reduce_scatter | solution.py:25
  899.0 75.8 %reduce-scatter.23.cloned.1.call-done = f32[64,128]{1,0:T(8,128)} async-done(((f32[64,2048]{1,0:T(8,128)}), f32[64,128]{1,0:T(8,128)}) %reduce-scatter.23.cloned.1.call-update) | async-done | bytes 32784 | tf_op jit(solution)/shard_map/reduce_scatter | solution.py:68
  975.7 84.6 %psum.31 = f32[64,64]{0,1:T(8,128)S(1)} all-reduce(f32[64,64]{0,1:T(8,128)S(1)} %fusion.67), channel_id=1, replica_groups=mesh['row'=16,'col'=16] {'row','col'}, use_global_device_ids=true, to_apply=%region_13.16 | all-reduce | flops 4096 | bytes 32768 | tf_op jit(solution)/shard_map/psum | solution.py:19
  (76 shorter events, 74.9 us)
Async XLA Ops:
  6.5 24.3 %copy-start = (f32[64,128]{1,0:T(8,128)S(1)}, f32[64,128]{1,0:T(8,128)}, u32[]{:S(2)}) copy-start(f32[64,128]{1,0:T(8,128)} %param.7) | copy-start | bytes 98308
  6.5 170.2 %reduce-scatter.25.cloned.1.call-start = ((), (), s32[]{:S(2)}) async-start(), calls=%async_computation.14 | async-start | bytes 1114112
  16.3 3.2 copy-start.1
  22.9 7.9 copy-start.2
  22.9 159.6 %reduce-scatter.27.cloned.1.call-start = ((), (), s32[]{:S(2)}) async-start(), calls=%async_computation.15 | async-start | bytes 1114112
  30.7 283.8 %reduce-scatter.13.cloned.1.call-start = ((), (), s32[]{:S(2)}) async-start(), calls=%async_computation.8 | async-start | bytes 557056 | tf_op jit(solution)/shard_map/reduce_scatter | solution.py:25
  223.1 166.5 %reduce-scatter.15.cloned.1.call-start = ((), (), s32[]{:S(2)}) async-start(), calls=%async_computation.9 | async-start | bytes 557056 | tf_op jit(solution)/shard_map/reduce_scatter | solution.py:68
  279.3 327.4 %reduce-scatter.17.cloned.1.call-start = ((), (), s32[]{:S(2)}) async-start(), calls=%async_computation.10 | async-start | bytes 557056 | tf_op jit(solution)/shard_map/reduce_scatter | solution.py:25
  529.2 152.2 %reduce-scatter.19.cloned.1.call-start = ((), (), s32[]{:S(2)}) async-start(), calls=%async_computation.11 | async-start | bytes 557056 | tf_op jit(solution)/shard_map/reduce_scatter | solution.py:68
  571.1 327.8 %reduce-scatter.21.cloned.1.call-start = ((), (), s32[]{:S(2)}) async-start(), calls=%async_computation.12 | async-start | bytes 557056 | tf_op jit(solution)/shard_map/reduce_scatter | solution.py:25
  821.4 153.3 %reduce-scatter.23.cloned.1.call-start = ((), (), s32[]{:S(2)}) async-start(), calls=%async_computation.13 | async-start | bytes 557056 | tf_op jit(solution)/shard_map/reduce_scatter | solution.py:68
Sparse Core Ops, SparseCore 0:
  23.1 81.6 reduce-scatter.24
  107.3 75.2 reduce-scatter.26
  223.2 91.2 reduce-scatter.12
  316.9 72.6 reduce-scatter.14
  529.3 77.3 reduce-scatter.16
  609.1 72.2 reduce-scatter.18
  821.5 77.3 reduce-scatter.20
  901.4 73.2 reduce-scatter.22
where the time goes:
time: 1080 us
  blocking collectives  561 us (52%)
  waiting for transfers between devices  337 us (31%)
  other arithmetic  59.2 us (5%)
  local copies, waits for them, and re-layouts  57.1 us (5%)
  matrix products  51.7 us (5%)
  between operations  13.8 us (1%)
    psum x4, blocking collectives, orthonormalize(): total_gram = lax.psum(partial_gram, ('row', 'col'))  338 us
    reduce_scatter x3, waiting for transfers between devices, mirror_sums(): return lax.psum_scatter(term, 'row', scatter_dimension=1, tiled=True)  225 us
    all_gather x3, blocking collectives, local(): lax.all_gather(vectors, 'col', axis=1, tiled=True)  122 us
    reduce_scatter x3, waiting for transfers between devices, collect_direct(): return lax.psum_scatter(term, 'col', scatter_dimension=1, tiled=True)  106 us
    all_gather x3, blocking collectives, direct_part(): lax.all_gather(vectors, 'row', axis=1, tiled=True)  101 us
    gather x1, local copies, waits for them, and re-layouts, local(): jnp.take_along_axis(start_vectors, jnp.broadcast_to(cluster_order, start_...  50.7 us
    another operation x12, other arithmetic, orthonormalize(): factor = jnp.linalg.cholesky(total_gram)  26.1 us
    another operation x8, other arithmetic, orthonormalize(): return jax.scipy.linalg.solve_triangular(factor, panel_in, lower=True)  22.2 us
  transfers between devices with their start and end apart: 8, of which 7 were waited for; matrix products, arithmetic and copies ran while one was open for 8% of the time, Pallas kernels for 0%

commit v1 on v0

v1 whole, which is shorter than its diff:
```python
import functools
import math

import jax
import jax.numpy as jnp
from jax import lax
from jax.experimental import pallas as pl
from jax.experimental.pallas import tpu as pltpu
from jax.sharding import PartitionSpec as P

ITERS = 3
K = 64
B = 128
NY, NL, NH, NX, NC = 4, 4, 2, 4, 2
MESH = pl.DeviceIdType.MESH
HI = lax.Precision.HIGHEST
F32 = jnp.float32
BF = jnp.bfloat16


def inverse_factor(packed):
    half = K // 2
    low = lax.broadcasted_iota(jnp.int32, (half, 2 * K), 1) < K
    row_id = lax.broadcasted_iota(jnp.int32, (half, 2 * K), 0)
    lane_id = lax.broadcasted_iota(jnp.int32, (half, 2 * K), 1)
    top = jnp.where(low, (row_id == lane_id).astype(F32), pltpu.roll(packed, K, 1))
    bottom = jnp.where(low, (row_id + half == lane_id).astype(F32), packed)
    rows = [top[8 * g : 8 * g + 8] for g in range(half // 8)]
    rows += [bottom[8 * g : 8 * g + 8] for g in range(half // 8)]
    sub = lax.broadcasted_iota(jnp.int32, (8, 2 * K), 0)
    groups = K // 8
    for j in range(K):
        first, s = divmod(j, 8)
        pivot_row = jnp.broadcast_to(rows[first][s : s + 1, :], (8, 2 * K))
        pivot = jnp.broadcast_to(pivot_row[:, K + j : K + j + 1], (8, 2 * K))
        scaled = pivot_row / pivot
        for g in range(first, groups):
            column = jnp.broadcast_to(rows[g][:, K + j : K + j + 1], (8, 2 * K))
            if g == first:
                if s == 7:
                    continue
                column = jnp.where(sub > s, column, 0.0)
            rows[g] = rows[g] - column * scaled
    out = []
    for g in range(groups):
        lane = lax.broadcasted_iota(jnp.int32, (8, 2 * K), 1)
        on_diag = lane == sub + (K + 8 * g)
        diag = jnp.sum(jnp.where(on_diag, rows[g], 0.0), axis=1, keepdims=True)
        out.append(rows[g] * (1.0 / jnp.sqrt(diag)))
    return jnp.concatenate(out, axis=0)[:, :K]


def kernel(
    start_ref,
    order_ref,
    mask_ref,
    w_ref,
    out_ref,
    matrix,
    wdiag,
    vsend,
    vrow,
    vcol,
    dsum,
    d1,
    d2,
    rc,
    rx,
    rz,
    msum,
    m1,
    ry,
    rl,
    edsum,
    ed1,
    ed2,
    erc,
    erx,
    erz,
    emsum,
    em1,
    ery,
    erl,
    gs,
    ga,
    gb,
    gy,
    gl,
    wsem,
    ssem,
    rsem,
):
    r = lax.axis_index("row")
    c = lax.axis_index("col")
    y, l = r // NL, r % NL
    h, e = c // (NX * NC), c % (NX * NC)
    x, core = e // NC, e % NC

    chunk_copies = []
    for a in range(16):
        cp = pltpu.make_async_copy(
            w_ref.at[pl.ds(a * B, B), :], matrix.at[pl.ds(a * B, B), :], wsem.at[a]
        )
        cp.start()
        chunk_copies.append(cp)
    diag_copy = pltpu.make_async_copy(
        w_ref.at[pl.ds(pl.multiple_of(c * B, B), B), pl.ds(pl.multiple_of(r * B, B), B)],
        wdiag,
        wsem.at[16],
    )
    diag_copy.start()

    barrier = pltpu.get_barrier_semaphore()
    for d in range(1, 16):
        pl.semaphore_signal(
            barrier, inc=1, device_id=(r, (c + d) % 16), device_id_type=MESH
        )
        pl.semaphore_signal(
            barrier, inc=1, device_id=((r + d) % 16, c), device_id_type=MESH
        )

    count = [0]
    pending = []

    def slot():
        count[0] += 1
        return count[0] - 1

    def send(src, dst, row, col, index):
        cp = pltpu.make_async_remote_copy(
            src_ref=src,
            dst_ref=dst,
            send_sem=ssem.at[index],
            recv_sem=rsem.at[index],
            device_id=(row, col),
            device_id_type=MESH,
        )
        cp.start()
        pending.append(cp)
        return cp

    def col_of(hh, ee):
        return hh * (NX * NC) + ee

    def row_of(yy, ll):
        return yy * NL + ll

    def gram_start(t, panel):
        gram = lax.dot_general(
            panel, panel, (((1,), (1,)), ((), ())), precision=HI, preferred_element_type=F32
        )
        gs[t, 0] = jnp.concatenate([gram[: K // 2], gram[K // 2 :]], axis=1)
        cps = []
        for d in range(1, NX * NC):
            cps.append(send(gs.at[t, 0], ga.at[t, d - 1], r, col_of(h, (e + d) % 8), slot()))
        return cps

    def gram_h(t, cps):
        for cp in cps:
            cp.wait_recv()
        total = gs[t, 0]
        for d in range(7):
            total = total + ga[t, d]
        gs[t, 1] = total
        return [send(gs.at[t, 1], gb.at[t], r, col_of(1 - h, e), slot())]

    def gram_y(t, cps):
        for cp in cps:
            cp.wait_recv()
        gs[t, 2] = gs[t, 1] + gb[t]
        out = []
        for d in range(1, NY):
            out.append(send(gs.at[t, 2], gy.at[t, d - 1], row_of((y + d) % NY, l), c, slot()))
        return out

    def gram_l(t, cps):
        for cp in cps:
            cp.wait_recv()
        gs[t, 3] = ((gs[t, 2] + gy[t, 0]) + gy[t, 1]) + gy[t, 2]
        out = []
        for d in range(1, NL):
            out.append(send(gs.at[t, 3], gl.at[t, d - 1], row_of(y, (l + d) % NL), c, slot()))
        return out

    def gram_end(t, cps):
        for cp in cps:
            cp.wait_recv()
        return inverse_factor(((gs[t, 3] + gl[t, 0]) + gl[t, 1]) + gl[t, 2])

    def rs_core(src, dst):
        return [send(src.at[1 - core], dst, r, col_of(h, x * NC + 1 - core), slot())]

    def rs_x(cps, src, got, mid, dst):
        for cp in cps:
            cp.wait_recv()
        mid[...] = src[core] + got[...]
        out = []
        for d in range(1, NX):
            xx = (x + d) % NX
            out.append(send(mid.at[xx], dst.at[d - 1], r, col_of(h, xx * NC + core), slot()))
        return out

    def rs_h(cps, mid, got, last, dst):
        for cp in cps:
            cp.wait_recv()
        last[...] = ((mid[x] + got[0]) + got[1]) + got[2]
        return [send(last.at[1 - h], dst, r, col_of(1 - h, e), slot())]

    def rs_y(src, dst):
        out = []
        for d in range(1, NY):
            yy = (y + d) % NY
            out.append(send(src.at[yy], dst.at[d - 1], row_of(yy, l), c, slot()))
        return out

    def rs_l(cps, src, got, mid, dst):
        for cp in cps:
            cp.wait_recv()
        mid[...] = ((src[y] + got[0]) + got[1]) + got[2]
        out = []
        for d in range(1, NL):
            ll = (l + d) % NL
            out.append(send(mid.at[ll], dst.at[d - 1], row_of(y, ll), c, slot()))
        return out

    def wait_all(cps):
        for cp in cps:
            cp.wait_recv()

    order = order_ref[...]
    pick = (lax.broadcasted_iota(jnp.int32, (B, B), 0) == jnp.broadcast_to(order, (B, B))).astype(F32)
    panel = jnp.dot(start_ref[...], pick, precision=HI, preferred_element_type=F32)
    pl.semaphore_wait(barrier, 30)
    gram_cps = gram_start(0, panel)

    spread = (
        lax.broadcasted_iota(jnp.int32, (16, 16 * B), 1) // B
        == lax.broadcasted_iota(jnp.int32, (16, 16 * B), 0)
    ).astype(F32)
    live = jnp.dot((mask_ref[...] > 0).astype(F32), spread, preferred_element_type=F32)
    col_block = lax.broadcasted_iota(jnp.int32, (1, 16 * B), 1) // B * 16 + c
    ones_wide = jnp.ones((8, 16 * B), BF)
    ones_rows = jnp.ones((8, B), BF)
    diag_copy.wait()
    upper = lax.broadcasted_iota(jnp.int32, (B, B), 0) < lax.broadcasted_iota(jnp.int32, (B, B), 1)
    diag_value = jnp.where(upper, wdiag[...].astype(F32), 0.0).astype(BF)
    col_totals = jnp.zeros((8, 16 * B), F32)
    for a in range(16):
        chunk_copies[a].wait()
        keep = jnp.where((live[a : a + 1, :] > 0.5) & (col_block > r * 16 + a), 1.0, 0.0).astype(BF)
        rows = pl.ds(a * B, B)
        matrix[rows, :] = matrix[rows, :] * jnp.broadcast_to(keep, (B, 16 * B))
    matrix[pl.ds(pl.multiple_of(c * B, B), B), pl.ds(pl.multiple_of(r * B, B), B)] = diag_value
    gram_cps = gram_h(0, gram_cps)
    for a in range(16):
        rows = pl.ds(a * B, B)
        block = matrix[rows, :]
        col_totals = col_totals + jnp.dot(ones_rows, block, preferred_element_type=F32)
        edsum[a % 2, a // 2 % 4, a // 8] = lax.dot_general(
            ones_wide, block, (((1,), (1,)), ((), ())), preferred_element_type=F32
        )
    for i in range(16):
        emsum[i // NL, i % NL] = col_totals[:, i * B : (i + 1) * B]
    cps_c = rs_core(edsum, erc)
    cps_r = rs_y(emsum, ery)
    cps_c = rs_x(cps_c, edsum, erc, ed1, erx)
    cps_r = rs_l(cps_r, emsum, ery, em1, erl)
    gram_cps = gram_y(0, gram_cps)
    cps_c = rs_h(cps_c, ed1, erx, ed2, erz)
    gram_cps = gram_l(0, gram_cps)
    wait_all(cps_r)
    wait_all(cps_c)
    degree = (ed2[h] + erz[...]) + (((em1[l] + erl[0]) + erl[1]) + erl[2])
    inverse_root = jnp.broadcast_to(1.0 / jnp.sqrt(degree[0:1, :]), (K, B))
    factor = gram_end(0, gram_cps)
    panel = jnp.dot(factor, panel, precision=HI, preferred_element_type=F32)

    for t in range(ITERS):
        vectors = (inverse_root * panel).astype(BF)
        vsend[t] = vectors
        vrow[t, c] = vectors
        vcol[t, r] = vectors
        own = vsend.at[t]
        cps_h = send(own, vrow.at[t, c], r, col_of(1 - h, e), slot())
        cps_l = []
        for d in range(1, NL):
            cps_l.append(send(own, vcol.at[t, r], row_of(y, (l + d) % NL), c, slot()))
        cps_e = []
        for d in range(1, 8):
            cps_e.append(send(own, vrow.at[t, c], r, col_of(h, (e + d) % 8), slot()))
        cps_y = []
        for d in range(1, NY):
            cps_y.append(send(own, vcol.at[t, r], row_of((y + d) % NY, l), c, slot()))
        if t > 0:
            gram_cps = gram_start(t, panel)
        for d in range(1, NL):
            cps_l[d - 1].wait_recv()
            from_l = row_of(y, (l - d + NL) % NL)
            for f in range(1, NY):
                cps_y.append(
                    send(vcol.at[t, from_l], vcol.at[t, from_l], row_of((y + f) % NY, l), c, slot())
                )
        cps_h.wait_recv()
        other = col_of(1 - h, e)
        for d in range(1, 8):
            cps_e.append(send(vrow.at[t, other], vrow.at[t, other], r, col_of(h, (e + d) % 8), slot()))
        if t > 0:
            gram_cps = gram_h(t, gram_cps)
        wait_all(cps_e)
        wide = jnp.concatenate([vrow[t, i] for i in range(16)], axis=1)

        def mirror_step(j, _):
            out = jnp.dot(
                wide,
                matrix[:, pl.ds(pl.multiple_of(j * 2 * B, 2 * B), 2 * B)],
                preferred_element_type=F32,
            )
            msum[t, j // 2, 2 * (j % 2)] = out[:, :B]
            msum[t, j // 2, 2 * (j % 2) + 1] = out[:, B:]
            return 0

        lax.fori_loop(0, 8, mirror_step, 0)
        cps_r = rs_y(msum.at[t], ry.at[t])
        if t > 0:
            gram_cps = gram_y(t, gram_cps)
        wait_all(cps_y)
        wide_c = jnp.concatenate([vcol[t, i] for i in range(16)], axis=1)

        def direct_step(j, _):
            out = lax.dot_general(
                wide_c,
                matrix[pl.ds(pl.multiple_of(j * 2 * B, 2 * B), 2 * B), :],
                (((1,), (1,)), ((), ())),
                preferred_element_type=F32,
            )
            dsum[t, 0, j % 4, j // 4] = out[:, :B]
            dsum[t, 1, j % 4, j // 4] = out[:, B:]
            return 0

        lax.fori_loop(0, 8, direct_step, 0)
        cps_c = rs_core(dsum.at[t], rc.at[t])
        if t > 0:
            gram_cps = gram_l(t, gram_cps)
        cps_c = rs_x(cps_c, dsum.at[t], rc.at[t], d1.at[t], rx.at[t])
        cps_r = rs_l(cps_r, msum.at[t], ry.at[t], m1.at[t], rl.at[t])
        cps_c = rs_h(cps_c, d1.at[t], rx.at[t], d2.at[t], rz.at[t])
        if t > 0:
            factor = gram_end(t, gram_cps)
        wait_all(cps_r)
        wait_all(cps_c)
        product = (d2[t, h] + rz[t]) + (((m1[t, l] + rl[t, 0]) + rl[t, 1]) + rl[t, 2])
        panel = panel + inverse_root * product
        if t > 0:
            panel = jnp.dot(factor, panel, precision=HI, preferred_element_type=F32)

    gram_cps = gram_start(ITERS, panel)
    gram_cps = gram_h(ITERS, gram_cps)
    gram_cps = gram_y(ITERS, gram_cps)
    gram_cps = gram_l(ITERS, gram_cps)
    factor = gram_end(ITERS, gram_cps)
    out_ref[...] = jnp.dot(factor, panel, precision=HI, preferred_element_type=F32)
    for cp in pending:
        cp.wait_send()


def copies():
    gram = 7 + 1 + 3 + 3
    scatter = 1 + 3 + 1 + 3 + 3
    gather = 1 + 3 + 7 + 3 + 9 + 7
    return (ITERS + 1) * (gram + scatter) + ITERS * gather


def local(start_vectors, cluster_order, weights, block_mask):
    vm = pltpu.VMEM
    n = ITERS
    blk = (K, B)
    eblk = (8, B)
    g = (K // 2, 2 * K)
    scratch = [
        vm((16 * B, 16 * B), BF),
        vm((B, B), BF),
        vm((n,) + blk, BF),
        vm((n, 16) + blk, BF),
        vm((n, 16) + blk, BF),
        vm((n, NC, NX, NH) + blk, F32),
        vm((n, NX, NH) + blk, F32),
        vm((n, NH) + blk, F32),
        vm((n, NX, NH) + blk, F32),
        vm((n, NX - 1, NH) + blk, F32),
        vm((n,) + blk, F32),
        vm((n, NY, NL) + blk, F32),
        vm((n, NL) + blk, F32),
        vm((n, NY - 1, NL) + blk, F32),
        vm((n, NL - 1) + blk, F32),
        vm((NC, NX, NH) + eblk, F32),
        vm((NX, NH) + eblk, F32),
        vm((NH,) + eblk, F32),
        vm((NX, NH) + eblk, F32),
        vm((NX - 1, NH) + eblk, F32),
        vm(eblk, F32),
        vm((NY, NL) + eblk, F32),
        vm((NL,) + eblk, F32),
        vm((NY - 1, NL) + eblk, F32),
        vm((NL - 1,) + eblk, F32),
        vm((n + 1, 4) + g, F32),
        vm((n + 1, 7) + g, F32),
        vm((n + 1,) + g, F32),
        vm((n + 1, 3) + g, F32),
        vm((n + 1, 3) + g, F32),
        pltpu.SemaphoreType.DMA((17,)),
        pltpu.SemaphoreType.DMA((copies(),)),
        pltpu.SemaphoreType.DMA((copies(),)),
    ]
    space = pl.BlockSpec(memory_space=pltpu.VMEM)
    panel = pl.pallas_call(
        kernel,
        out_shape=jax.ShapeDtypeStruct(blk, F32),
        in_specs=[space, space, space, pl.BlockSpec(memory_space=pltpu.HBM)],
        out_specs=space,
        scratch_shapes=scratch,
        compiler_params=pltpu.CompilerParams(
            collective_id=0, has_side_effects=True, vmem_limit_bytes=48 * 1024 * 1024
        ),
    )(start_vectors, cluster_order, block_mask[:, 0, :], weights[:, 0, :])
    return math.sqrt(16 * 16 * B) * panel


def solution(mesh):
    placed = (
        P(None, ("row", "col")),
        P(("row", "col"), None),
        P("row", "col", None),
        P("row", "col", None),
    )
    return jax.shard_map(
        local, mesh=mesh, in_specs=placed, out_specs=P(None, ("row", "col")), check_vma=False
    )
```

time: 1080 us -> 163 us (0.15)
  blocking collectives: 561 us -> 0 us
  waiting for transfers between devices: 337 us -> 0 us
  Pallas kernels: 0 us -> 159 us
  other arithmetic: 59.2 us -> 0.62 us
  local copies, waits for them, and re-layouts: 57.1 us -> 2.11 us
  matrix products: 51.7 us -> 0 us
  between operations: 13.8 us -> 0.01 us
    psum x4 -> x0, blocking collectives: 338 us -> none  [orthonormalize(): total_gram = lax.psum(partial_gram, ('row', 'col'))]
    reduce_scatter x6 -> x0, waiting for transfers between devices: 332 us -> none  [the longest x3 225 us: mirror_sums(): return lax.psum_scatter(term, 'row', scatter_dimension=1, tiled=True)]
    all_gather x6 -> x0, blocking collectives: 223 us -> none  [the longest x3 122 us: local(): lax.all_gather(vectors, 'col', axis=1, tiled=True)]
    pallas_call x0 -> x1, Pallas kernels: none -> 159 us  [local(): pl.pallas_call(kernel, out_shape=jax.ShapeDtypeStruct(blk, F32), in_specs...]
    gather x1 -> x0, local copies, waits for them, and re-layouts: 50.7 us -> none  [local(): jnp.take_along_axis(start_vectors, jnp.broadcast_to(cluster_order, start_...]
    another operation x20 -> x0, other arithmetic: 48.3 us -> none  [the longest x12 26.1 us: orthonormalize(): factor = jnp.linalg.cholesky(total_gram)]
    dot_general x10 -> x0, matrix products: 38.9 us -> none  [the longest x3 20.7 us: direct_part(): lax.dot_general(lax.all_gather(vectors, 'row', axis=1, tiled=True), matri...]
    unnamed x2 -> x0, matrix products: 11.2 us -> none
  transfers between devices with their start and end apart: 8 -> 0, of which waited for: 7 -> 0; matrix products, arithmetic and copies ran while one was open for 8% -> 0% of each run, Pallas kernels for 0% -> 0%
where the time goes in v1:
time: 163 us; the launch traced here: 162 us
  Pallas kernels  159 us (98%)
  local copies, waits for them, and re-layouts  2.11 us (1%)
    pallas_call x1, Pallas kernels, local(): pl.pallas_call(kernel, out_shape=jax.ShapeDtypeStruct(blk, F32), in_specs...  159 us

profile of v1, /device:TPU:1, one launch (start us, length us, event | category | flops | bytes accessed | tf_op | source)
XLA Modules:
  0.0 162.2 jit_solution(5251800424008917632)
XLA Ops:
  0.0 0.0 copy-start
  0.0 0.8 copy-done
  0.8 0.0 copy-start.1
  0.8 0.7 copy-done.1
  1.5 0.0 copy-start.2
  1.5 0.7 copy-done.2
  2.1 159.5 %shard_map.46 = f32[64,128]{1,0:T(8,128)S(1)} custom-call(f32[64,128]{1,0:T(8,128)S(1)} %copy-done, s32[1,128]{1,0:T(1,128)S(1)} %copy-done.2, s32[16,16]{1,0:T(8,128)S(1)} %bitcast.2, bf16[2048,2048]{1,0:T(8,128)(2,1)} %bitcast.3), custom_call_target="tpu_custom_call" | custom-call | tf_op jit(solution)/shard_map/pallas_call | solution.py:415
  161.6 0.6 broadcast_multiply_fusion
Async XLA Ops:
  0.0 0.8 copy-start
  0.8 0.7 copy-start.1
  1.5 0.7 copy-start.2

commit v2 on v1

v2 whole, which is shorter than its diff:
```python
import functools
import math

import jax
import jax.numpy as jnp
from jax import lax
from jax.experimental import pallas as pl
from jax.experimental.pallas import tpu as pltpu
from jax.sharding import PartitionSpec as P

ITERS = 3
K = 64
B = 128
NY, NL, NH, NX, NC = 4, 4, 2, 4, 2
MESH = pl.DeviceIdType.MESH
HI = lax.Precision.HIGHEST
F32 = jnp.float32
BF = jnp.bfloat16


def inverse_factor(blocks):
    groups = K // 8
    lane = lax.broadcasted_iota(jnp.int32, (8, 2 * K), 1)
    sub = lax.broadcasted_iota(jnp.int32, (8, 2 * K), 0)
    rows = [
        jnp.where(lane < K, (lane == sub + 8 * g).astype(F32), blocks[g]) for g in range(groups)
    ]

    def row_of_all(value, k):
        return jnp.broadcast_to(value[k : k + 1, :], (8, 2 * K))

    def column_of_all(value, j):
        return jnp.broadcast_to(value[:, K + j : K + j + 1], (8, 2 * K))

    out = []
    for b in range(groups):
        block = rows[b]
        columns = [column_of_all(block, 8 * b + m) for m in range(8)]
        pivots = {(k, m): row_of_all(columns[m], k) for m in range(8) for k in range(m, 8)}
        lower, inverses, reduced = {}, [], []
        for m in range(8):
            inverses.append(1.0 / pivots[m, m])
            for k in range(m + 1, 8):
                lower[k, m] = pivots[k, m] * inverses[m]
            for k in range(m + 1, 8):
                for n in range(m + 1, k + 1):
                    pivots[k, n] = pivots[k, n] - lower[k, m] * pivots[n, m]
        for k in range(8):
            value = row_of_all(block, k)
            for m in range(k):
                value = value - lower[k, m] * reduced[m]
            reduced.append(value)
        if b + 1 < groups:
            solved = [None] * 8
            for k in reversed(range(8)):
                value = reduced[k] * inverses[k]
                for n in range(k + 1, 8):
                    value = value - lower[n, k] * solved[n]
                solved[k] = value
            for g in range(b + 1, groups):
                value = rows[g]
                for k in range(8):
                    value = value - column_of_all(rows[g], 8 * b + k) * solved[k]
                rows[g] = value
        result = jnp.zeros((8, 2 * K), F32)
        for k in range(8):
            result = jnp.where(sub == k, reduced[k] * (1.0 / jnp.sqrt(pivots[k, k])), result)
        out.append(result)
    return jnp.concatenate(out, axis=0)[:, :K]


def kernel(
    start_hbm,
    order_hbm,
    mask_hbm,
    w_ref,
    out_ref,
    start_ref,
    order_ref,
    mask_ref,
    matrix,
    wdiag,
    vsend,
    vrow,
    vcol,
    dsum,
    d1,
    d2,
    rc,
    xq,
    xm,
    rz,
    msum,
    m1,
    yq,
    ym,
    rl,
    edsum,
    ed1,
    ed2,
    erc,
    erx,
    erz,
    emsum,
    em1,
    ery,
    erl,
    gs,
    ga,
    g1,
    gy,
    g2,
    gz,
    gf,
    wsem,
    ssem,
    rsem,
):
    r = lax.axis_index("row")
    c = lax.axis_index("col")
    y, l = r // NL, r % NL
    h, e = c // (NX * NC), c % (NX * NC)
    x, core = e // NC, e % NC
    z = h * NL + l
    rest = NX * NC

    def col_of(hh, ee):
        return hh * rest + ee

    def row_of(yy, ll):
        return yy * NL + ll

    barrier = pltpu.get_barrier_semaphore()
    for d in range(1, NH * NL):
        zz = (z + d) % (NH * NL)
        pl.semaphore_signal(
            barrier,
            inc=1,
            device_id=(row_of(y, zz % NL), col_of(zz // NL, e)),
            device_id_type=MESH,
        )
    for d in range(1, NY):
        pl.semaphore_signal(
            barrier, inc=1, device_id=(row_of((y + d) % NY, l), c), device_id_type=MESH
        )
    for d in range(1, rest):
        pl.semaphore_signal(
            barrier, inc=1, device_id=(r, col_of(h, (e + d) % rest)), device_id_type=MESH
        )

    local_copies = []
    for i, (src, dst) in enumerate(
        ((order_hbm, order_ref), (start_hbm, start_ref), (mask_hbm, mask_ref))
    ):
        cp = pltpu.make_async_copy(src, dst, wsem.at[17 + i])
        cp.start()
        local_copies.append(cp)
    chunk_copies = []
    for a in range(16):
        cp = pltpu.make_async_copy(
            w_ref.at[pl.ds(a * B, B), :], matrix.at[pl.ds(a * B, B), :], wsem.at[a]
        )
        cp.start()
        chunk_copies.append(cp)
    diag_copy = pltpu.make_async_copy(
        w_ref.at[pl.ds(pl.multiple_of(c * B, B), B), pl.ds(pl.multiple_of(r * B, B), B)],
        wdiag,
        wsem.at[16],
    )
    diag_copy.start()

    count = [0]
    pending = []

    def send(src, dst, row, col):
        index = count[0]
        count[0] += 1
        cp = pltpu.make_async_remote_copy(
            src_ref=src,
            dst_ref=dst,
            send_sem=ssem.at[index],
            recv_sem=rsem.at[index],
            device_id=(row, col),
            device_id_type=MESH,
        )
        cp.start()
        pending.append(cp)
        return cp

    def wait_all(cps):
        for cp in cps:
            cp.wait_recv()

    def gram_local(t, panel):
        padded = jnp.concatenate([jnp.zeros((K, B), F32), panel], axis=0)
        gram = lax.dot_general(
            panel, padded, (((1,), (1,)), ((), ())), precision=HI, preferred_element_type=F32
        )
        for g in range(8):
            gs[t, g] = gram[8 * g : 8 * g + 8]

    def gram_start(t):
        return [
            send(gs.at[t, (e + d) % rest], ga.at[t, d - 1], r, col_of(h, (e + d) % rest))
            for d in range(1, rest)
        ]

    def gram_y(t, cps):
        wait_all(cps)
        total = gs[t, e]
        for d in range(rest - 1):
            total = total + ga[t, d]
        g1[t] = total
        return [
            send(g1.at[t], gy.at[t, d - 1], row_of((y + d) % NY, l), c) for d in range(1, NY)
        ]

    def gram_z(t, cps):
        wait_all(cps)
        g2[t] = ((g1[t] + gy[t, 0]) + gy[t, 1]) + gy[t, 2]
        out = []
        for d in range(1, NH * NL):
            zz = (z + d) % (NH * NL)
            out.append(send(g2.at[t], gz.at[t, d - 1], row_of(y, zz % NL), col_of(zz // NL, e)))
        return out

    def gram_all(t, cps):
        wait_all(cps)
        total = g2[t]
        for d in range(NH * NL - 1):
            total = total + gz[t, d]
        gf[t, e] = total
        return [
            send(gf.at[t, e], gf.at[t, e], r, col_of(h, (e + d) % rest)) for d in range(1, rest)
        ]

    def gram_end(t, cps):
        wait_all(cps)
        return inverse_factor([gf[t, g] for g in range(8)])

    def rs_core(src, dst):
        return [send(src.at[1 - core], dst, r, col_of(h, x * NC + 1 - core))]

    def rs_h(last, dst):
        return [send(last.at[1 - h], dst, r, col_of(1 - h, e))]

    def rs_l(mid, dst):
        out = []
        for d in range(1, NL):
            ll = (l + d) % NL
            out.append(send(mid.at[ll], dst.at[d - 1], row_of(y, ll), c))
        return out

    first, second = pl.ds(0, K // 2), pl.ds(K // 2, K // 2)

    def ring_start(src, q, p, device):
        ahead, behind, across = (p + 1) % 4, (p + 3) % 4, (p + 2) % 4
        return [
            send(src.at[across, :, first, :], q.at[0], *device(ahead)),
            send(src.at[across, :, second, :], q.at[1], *device(behind)),
            send(src.at[ahead, :, second, :], q.at[2], *device(ahead)),
            send(src.at[behind, :, first, :], q.at[3], *device(behind)),
        ]

    def ring_mid(cps, src, q, mid, p, device):
        ahead, behind = (p + 1) % 4, (p + 3) % 4
        cps[0].wait_recv()
        mid[0] = src[ahead, :, first, :] + q[0]
        forth = send(mid.at[0], q.at[4], *device(ahead))
        cps[1].wait_recv()
        mid[1] = src[behind, :, second, :] + q[1]
        back = send(mid.at[1], q.at[5], *device(behind))
        return cps[2:] + [forth, back]

    def ring_end(cps, src, q, p, dst):
        wait_all(cps)
        dst[:, first, :] = (src[p, :, first, :] + q[3]) + q[4]
        dst[:, second, :] = (src[p, :, second, :] + q[2]) + q[5]

    def device_x(p):
        return r, col_of(h, p * NC + core)

    def device_y(p):
        return row_of(p, l), c

    local_copies[0].wait()
    local_copies[1].wait()
    pick = (
        lax.broadcasted_iota(jnp.int32, (B, B), 0) == jnp.broadcast_to(order_ref[...], (B, B))
    ).astype(F32)
    panel = jnp.dot(start_ref[...], pick, precision=HI, preferred_element_type=F32)
    gram_local(0, panel)

    local_copies[2].wait()
    mask = jnp.concatenate([mask_ref[a] for a in range(16)], axis=0)
    spread = (
        lax.broadcasted_iota(jnp.int32, (16, 16 * B), 1) // B
        == lax.broadcasted_iota(jnp.int32, (16, 16 * B), 0)
    ).astype(F32)
    live = jnp.dot((mask > 0).astype(F32), spread, preferred_element_type=F32)
    col_block = lax.broadcasted_iota(jnp.int32, (1, 16 * B), 1) // B * 16 + c
    ones_wide = jnp.ones((8, 16 * B), BF)
    ones_rows = jnp.ones((8, B), BF)
    col_totals = jnp.zeros((8, 16 * B), F32)
    for a in range(16):
        chunk_copies[a].wait()
        keep = jnp.where((live[a : a + 1, :] > 0.5) & (col_block > r * 16 + a), 1.0, 0.0)
        rows = pl.ds(a * B, B)
        block = matrix[rows, :] * jnp.broadcast_to(keep.astype(BF), (B, 16 * B))
        matrix[rows, :] = block
        col_totals = col_totals + jnp.dot(ones_rows, block, preferred_element_type=F32)
        edsum[a % 2, a // 2 % 4, a // 8] = lax.dot_general(
            ones_wide, block, (((1,), (1,)), ((), ())), preferred_element_type=F32
        )
    for i in range(16):
        emsum[i // NL, i % NL] = col_totals[:, i * B : (i + 1) * B]
    diag_copy.wait()
    upper = lax.broadcasted_iota(jnp.int32, (B, B), 0) < lax.broadcasted_iota(jnp.int32, (B, B), 1)
    diag_value = jnp.where(upper, wdiag[...].astype(F32), 0.0).astype(BF)
    matrix[pl.ds(pl.multiple_of(c * B, B), B), pl.ds(pl.multiple_of(r * B, B), B)] = diag_value
    diag_degree = jnp.dot(ones_rows, diag_value, preferred_element_type=F32) + lax.dot_general(
        ones_rows, diag_value, (((1,), (1,)), ((), ())), preferred_element_type=F32
    )

    pl.semaphore_wait(barrier, NH * NL - 1 + NY - 1 + rest - 1)
    gram_cps = gram_start(0)
    cps_c = rs_core(edsum, erc)
    cps_r = [
        send(emsum.at[(y + d) % NY], ery.at[d - 1], row_of((y + d) % NY, l), c)
        for d in range(1, NY)
    ]
    wait_all(cps_c)
    ed1[...] = edsum[core] + erc[...]
    cps_c = [
        send(ed1.at[(x + d) % NX], erx.at[d - 1], *device_x((x + d) % NX)) for d in range(1, NX)
    ]
    gram_cps = gram_y(0, gram_cps)
    wait_all(cps_r)
    em1[...] = ((emsum[y] + ery[0]) + ery[1]) + ery[2]
    cps_r = rs_l(em1, erl)
    wait_all(cps_c)
    ed2[...] = ((ed1[x] + erx[0]) + erx[1]) + erx[2]
    cps_c = rs_h(ed2, erz)
    gram_cps = gram_z(0, gram_cps)
    wait_all(cps_r)
    wait_all(cps_c)
    degree = (ed2[h] + erz[...]) + (((em1[l] + erl[0]) + erl[1]) + erl[2]) + diag_degree
    inverse_root = jnp.broadcast_to(1.0 / jnp.sqrt(degree[0:1, :]), (K, B))
    gram_cps = gram_all(0, gram_cps)
    factor = gram_end(0, gram_cps)
    panel = jnp.dot(factor, panel, precision=HI, preferred_element_type=F32)

    half = 8 * B
    quarter = 4 * B
    pair = 2 * B

    for t in range(ITERS):
        vectors = (inverse_root * panel).astype(BF)
        vsend[t] = vectors
        vrow[t, c] = vectors
        vcol[t, r] = vectors
        own = vsend.at[t]
        cps_h = send(own, vrow.at[t, c], r, col_of(1 - h, e))
        cps_l = [
            send(own, vcol.at[t, r], row_of(y, (l + d) % NL), c) for d in range(1, NL)
        ]
        cps_e = [
            send(own, vrow.at[t, c], r, col_of(h, (e + d) % rest)) for d in range(1, rest)
        ]
        cps_y = [
            send(own, vcol.at[t, r], row_of((y + d) % NY, l), c) for d in range(1, NY)
        ]
        if t > 0:
            gram_local(t, panel)
            gram_cps = gram_start(t)
        for d in range(1, NL):
            cps_l[d - 1].wait_recv()
            got = vcol.at[t, row_of(y, (l - d + NL) % NL)]
            for f in range(1, NY):
                cps_y.append(send(got, got, row_of((y + f) % NY, l), c))
        cps_h.wait_recv()
        got = vrow.at[t, col_of(1 - h, e)]
        cps_far = [send(got, got, r, col_of(h, (e + d) % rest)) for d in range(1, rest)]
        if t > 0:
            gram_cps = gram_y(t, gram_cps)

        wait_all(cps_e)
        near = jnp.concatenate([vrow[t, h * rest + i] for i in range(rest)], axis=1)

        def mirror_near(j, _):
            cols = pl.ds(pl.multiple_of(j * pair, pair), pair)
            out = jnp.dot(
                near,
                matrix[pl.ds(pl.multiple_of(h * half, half), half), cols],
                preferred_element_type=F32,
            )
            msum[t, j // 2, 2 * (j % 2)] = out[:, :B]
            msum[t, j // 2, 2 * (j % 2) + 1] = out[:, B:]
            return 0

        lax.fori_loop(0, 8, mirror_near, 0)
        own_y = jnp.concatenate([vcol[t, y * NL + i] for i in range(NL)], axis=1)

        def direct_near(j, _):
            rows = pl.ds(pl.multiple_of(j * pair, pair), pair)
            out = lax.dot_general(
                own_y,
                matrix[rows, pl.ds(pl.multiple_of(y * quarter, quarter), quarter)],
                (((1,), (1,)), ((), ())),
                preferred_element_type=F32,
            )
            dsum[t, 0, j % 4, j // 4] = out[:, :B]
            dsum[t, 1, j % 4, j // 4] = out[:, B:]
            return 0

        lax.fori_loop(0, 8, direct_near, 0)
        if t > 0:
            gram_cps = gram_z(t, gram_cps)
        wait_all(cps_y)
        others = []
        for d in range(1, NY):
            yy = (y + d) % NY
            others.append(
                (yy, jnp.concatenate([vcol[t, yy * NL + i] for i in range(NL)], axis=1))
            )

        def direct_far(j, _):
            rows = pl.ds(pl.multiple_of(j * pair, pair), pair)
            out = 0.0
            for yy, values in others:
                out = out + lax.dot_general(
                    values,
                    matrix[rows, pl.ds(pl.multiple_of(yy * quarter, quarter), quarter)],
                    (((1,), (1,)), ((), ())),
                    preferred_element_type=F32,
                )
            dsum[t, 0, j % 4, j // 4] += out[:, :B]
            dsum[t, 1, j % 4, j // 4] += out[:, B:]
            return 0

        lax.fori_loop(0, 8, direct_far, 0)
        cps_c = rs_core(dsum.at[t], rc.at[t])
        wait_all(cps_far)
        far = jnp.concatenate([vrow[t, (1 - h) * rest + i] for i in range(rest)], axis=1)

        def mirror_far(j, _):
            cols = pl.ds(pl.multiple_of(j * pair, pair), pair)
            out = jnp.dot(
                far,
                matrix[pl.ds(pl.multiple_of((1 - h) * half, half), half), cols],
                preferred_element_type=F32,
            )
            msum[t, j // 2, 2 * (j % 2)] += out[:, :B]
            msum[t, j // 2, 2 * (j % 2) + 1] += out[:, B:]
            return 0

        lax.fori_loop(0, 8, mirror_far, 0)
        cps_r = ring_start(msum.at[t], yq.at[t], y, device_y)
        wait_all(cps_c)
        d1[t] = dsum[t, core] + rc[t]
        cps_c = ring_start(d1.at[t], xq.at[t], x, device_x)
        if t > 0:
            gram_cps = gram_all(t, gram_cps)
        cps_c = ring_mid(cps_c, d1.at[t], xq.at[t], xm.at[t], x, device_x)
        cps_r = ring_mid(cps_r, msum.at[t], yq.at[t], ym.at[t], y, device_y)
        ring_end(cps_c, d1.at[t], xq.at[t], x, d2.at[t])
        cps_c = rs_h(d2.at[t], rz.at[t])
        ring_end(cps_r, msum.at[t], yq.at[t], y, m1.at[t])
        cps_r = rs_l(m1.at[t], rl.at[t])
        if t > 0:
            factor = gram_end(t, gram_cps)
        wait_all(cps_r)
        wait_all(cps_c)
        product = (d2[t, h] + rz[t]) + (((m1[t, l] + rl[t, 0]) + rl[t, 1]) + rl[t, 2])
        panel = panel + inverse_root * product
        if t > 0:
            panel = jnp.dot(factor, panel, precision=HI, preferred_element_type=F32)

    gram_local(ITERS, panel)
    gram_cps = gram_start(ITERS)
    gram_cps = gram_y(ITERS, gram_cps)
    gram_cps = gram_z(ITERS, gram_cps)
    gram_cps = gram_all(ITERS, gram_cps)
    factor = gram_end(ITERS, gram_cps)
    out_ref[...] = jnp.dot(factor, panel, precision=HI, preferred_element_type=F32)
    for cp in pending:
        cp.wait_send()


def copies():
    gram = 7 + 3 + 7 + 7
    degrees = 1 + 3 + 1 + 3 + 3
    scatter = 1 + 6 + 1 + 6 + 3
    gather = 1 + 3 + 7 + 3 + 9 + 7
    return (ITERS + 1) * gram + degrees + ITERS * (scatter + gather)


def local(start_vectors, cluster_order, weights, block_mask):
    vm = pltpu.VMEM
    n = ITERS
    blk = (K, B)
    hblk = (K // 2, B)
    eblk = (8, B)
    scratch = [
        vm(blk, F32),
        vm((1, B), jnp.int32),
        vm((16, 1, 16), jnp.int32),
        vm((16 * B, 16 * B), BF),
        vm((B, B), BF),
        vm((n,) + blk, BF),
        vm((n, 16) + blk, BF),
        vm((n, 16) + blk, BF),
        vm((n, NC, NX, NH) + blk, F32),
        vm((n, NX, NH) + blk, F32),
        vm((n, NH) + blk, F32),
        vm((n, NX, NH) + blk, F32),
        vm((n, 6, NH) + hblk, F32),
        vm((n, 2, NH) + hblk, F32),
        vm((n,) + blk, F32),
        vm((n, NY, NL) + blk, F32),
        vm((n, NL) + blk, F32),
        vm((n, 6, NL) + hblk, F32),
        vm((n, 2, NL) + hblk, F32),
        vm((n, NL - 1) + blk, F32),
        vm((NC, NX, NH) + eblk, F32),
        vm((NX, NH) + eblk, F32),
        vm((NH,) + eblk, F32),
        vm((NX, NH) + eblk, F32),
        vm((NX - 1, NH) + eblk, F32),
        vm(eblk, F32),
        vm((NY, NL) + eblk, F32),
        vm((NL,) + eblk, F32),
        vm((NY - 1, NL) + eblk, F32),
        vm((NL - 1,) + eblk, F32),
        vm((n + 1, 8) + eblk, F32),
        vm((n + 1, 7) + eblk, F32),
        vm((n + 1,) + eblk, F32),
        vm((n + 1, 3) + eblk, F32),
        vm((n + 1,) + eblk, F32),
        vm((n + 1, 7) + eblk, F32),
        vm((n + 1, 8) + eblk, F32),
        pltpu.SemaphoreType.DMA((20,)),
        pltpu.SemaphoreType.DMA((copies(),)),
        pltpu.SemaphoreType.DMA((copies(),)),
    ]
    hbm = pl.BlockSpec(memory_space=pltpu.HBM)
    panel = pl.pallas_call(
        kernel,
        out_shape=jax.ShapeDtypeStruct(blk, F32),
        in_specs=[hbm] * 4,
        out_specs=pl.BlockSpec(memory_space=pltpu.VMEM),
        scratch_shapes=scratch,
        compiler_params=pltpu.CompilerParams(
            collective_id=0, has_side_effects=True, vmem_limit_bytes=66 * 1000 * 1000
        ),
    )(start_vectors, cluster_order, block_mask, weights[:, 0, :])
    return math.sqrt(16 * 16 * B) * panel


def solution(mesh):
    placed = (
        P(None, ("row", "col")),
        P(("row", "col"), None),
        P("row", "col", None),
        P("row", "col", None),
    )
    return jax.shard_map(
        local, mesh=mesh, in_specs=placed, out_specs=P(None, ("row", "col")), check_vma=False
    )
```

time: 163 us -> 137 us (0.84)
  Pallas kernels: 159 us -> 136 us
  local copies, waits for them, and re-layouts: 2.11 us -> 0 us
    pallas_call x1, Pallas kernels: 159 us -> 136 us  [local(): pl.pallas_call(kernel, out_shape=jax.ShapeDtypeStruct(blk, F32), in_specs...]
    unnamed x6 -> x0, local copies, waits for them, and re-layouts: 2.11 us -> none
where the time goes in v2:
time: 137 us
  Pallas kernels  136 us (99%)
  other arithmetic  1.38 us (1%)
    pallas_call x1, Pallas kernels, local(): pl.pallas_call(kernel, out_shape=jax.ShapeDtypeStruct(blk, F32), in_specs...  136 us

profile of v2, /device:TPU:1, one launch (start us, length us, event | category | flops | bytes accessed | tf_op | source)
XLA Modules:
  0.0 137.0 jit_solution(8634205282444554674)
XLA Ops:
  0.0 135.6 %shard_map.46 = f32[64,128]{1,0:T(8,128)} custom-call(f32[64,128]{1,0:T(8,128)} %start_hbm.1, s32[1,128]{1,0:T(1,128)} %order_hbm.1, s32[16,1,16]{2,1,0:T(1,128)} %mask_hbm.1, bf16[2048,2048]{1,0:T(8,128)(2,1)} %bitcast.1), custom_call_target="tpu_custom_call" | custom-call | tf_op jit(solution)/shard_map/pallas_call | solution.py:547
  135.6 1.4 %broadcast_multiply_fusion = f32[64,128]{1,0:T(8,128)} fusion(f32[64,128]{1,0:T(8,128)} %shard_map.46), kind=kLoop, calls=%fused_computation | loop fusion | flops 8192 | bytes 65536 | tf_op jit(solution)/shard_map/mul | solution.py:557

commit v3 on v2

--- a/solution.py
+++ b/solution.py
@@ -11,6 +11,8 @@
 ITERS = 3
 K = 64
 B = 128
+GROUP = 4
+STEP = 8
 NY, NL, NH, NX, NC = 4, 4, 2, 4, 2
 MESH = pl.DeviceIdType.MESH
 HI = lax.Precision.HIGHEST
@@ -300,59 +302,75 @@
     live = jnp.dot((mask > 0).astype(F32), spread, preferred_element_type=F32)
     col_block = lax.broadcasted_iota(jnp.int32, (1, 16 * B), 1) // B * 16 + c
     ones_wide = jnp.ones((8, 16 * B), BF)
-    ones_rows = jnp.ones((8, B), BF)
+    ones_rows = jnp.ones((8, GROUP * B), BF)
     col_totals = jnp.zeros((8, 16 * B), F32)
-    for a in range(16):
-        chunk_copies[a].wait()
-        keep = jnp.where((live[a : a + 1, :] > 0.5) & (col_block > r * 16 + a), 1.0, 0.0)
-        rows = pl.ds(a * B, B)
-        block = matrix[rows, :] * jnp.broadcast_to(keep.astype(BF), (B, 16 * B))
+    group = GROUP
+    for a in range(0, 16, group):
+        for i in range(group):
+            chunk_copies[a + i].wait()
+        keep = jnp.concatenate(
+            [
+                jnp.broadcast_to(
+                    jnp.where(
+                        (live[a + i : a + i + 1, :] > 0.5) & (col_block > r * 16 + a + i), 1.0, 0.0
+                    ).astype(BF),
+                    (B, 16 * B),
+                )
+                for i in range(group)
+            ],
+            axis=0,
+        )
+        rows = pl.ds(a * B, group * B)
+        block = matrix[rows, :] * keep
         matrix[rows, :] = block
         col_totals = col_totals + jnp.dot(ones_rows, block, preferred_element_type=F32)
-        edsum[a % 2, a // 2 % 4, a // 8] = lax.dot_general(
+        totals = lax.dot_general(
             ones_wide, block, (((1,), (1,)), ((), ())), preferred_element_type=F32
         )
+        for i in range(group):
+            edsum[(a + i) % 2, (a + i) // 2 % 4, (a + i) // 8] = totals[:, i * B : (i + 1) * B]
+        if a == 0:
+            pl.semaphore_wait(barrier, NH * NL - 1 + NY - 1 + rest - 1)
+            gram_cps = gram_start(0)
     for i in range(16):
         emsum[i // NL, i % NL] = col_totals[:, i * B : (i + 1) * B]
     diag_copy.wait()
     upper = lax.broadcasted_iota(jnp.int32, (B, B), 0) < lax.broadcasted_iota(jnp.int32, (B, B), 1)
     diag_value = jnp.where(upper, wdiag[...].astype(F32), 0.0).astype(BF)
     matrix[pl.ds(pl.multiple_of(c * B, B), B), pl.ds(pl.multiple_of(r * B, B), B)] = diag_value
-    diag_degree = jnp.dot(ones_rows, diag_value, preferred_element_type=F32) + lax.dot_general(
-        ones_rows, diag_value, (((1,), (1,)), ((), ())), preferred_element_type=F32
+    diag_degree = jnp.dot(ones_rows[:, :B], diag_value, preferred_element_type=F32) + lax.dot_general(
+        ones_rows[:, :B], diag_value, (((1,), (1,)), ((), ())), preferred_element_type=F32
     )
 
-    pl.semaphore_wait(barrier, NH * NL - 1 + NY - 1 + rest - 1)
-    gram_cps = gram_start(0)
     cps_c = rs_core(edsum, erc)
     cps_r = [
         send(emsum.at[(y + d) % NY], ery.at[d - 1], row_of((y + d) % NY, l), c)
         for d in range(1, NY)
     ]
+    gram_cps = gram_y(0, gram_cps)
     wait_all(cps_c)
     ed1[...] = edsum[core] + erc[...]
     cps_c = [
         send(ed1.at[(x + d) % NX], erx.at[d - 1], *device_x((x + d) % NX)) for d in range(1, NX)
     ]
-    gram_cps = gram_y(0, gram_cps)
     wait_all(cps_r)
     em1[...] = ((emsum[y] + ery[0]) + ery[1]) + ery[2]
     cps_r = rs_l(em1, erl)
+    gram_cps = gram_z(0, gram_cps)
     wait_all(cps_c)
     ed2[...] = ((ed1[x] + erx[0]) + erx[1]) + erx[2]
     cps_c = rs_h(ed2, erz)
-    gram_cps = gram_z(0, gram_cps)
+    gram_cps = gram_all(0, gram_cps)
     wait_all(cps_r)
     wait_all(cps_c)
     degree = (ed2[h] + erz[...]) + (((em1[l] + erl[0]) + erl[1]) + erl[2]) + diag_degree
     inverse_root = jnp.broadcast_to(1.0 / jnp.sqrt(degree[0:1, :]), (K, B))
-    gram_cps = gram_all(0, gram_cps)
     factor = gram_end(0, gram_cps)
     panel = jnp.dot(factor, panel, precision=HI, preferred_element_type=F32)
 
     half = 8 * B
     quarter = 4 * B
-    pair = 2 * B
+    wide = STEP * B
 
     for t in range(ITERS):
         vectors = (inverse_root * panel).astype(BF)
@@ -388,74 +406,83 @@
         near = jnp.concatenate([vrow[t, h * rest + i] for i in range(rest)], axis=1)
 
         def mirror_near(j, _):
-            cols = pl.ds(pl.multiple_of(j * pair, pair), pair)
+            cols = pl.ds(pl.multiple_of(j * wide, wide), wide)
             out = jnp.dot(
                 near,
                 matrix[pl.ds(pl.multiple_of(h * half, half), half), cols],
                 preferred_element_type=F32,
             )
-            msum[t, j // 2, 2 * (j % 2)] = out[:, :B]
-            msum[t, j // 2, 2 * (j % 2) + 1] = out[:, B:]
+            for i in range(STEP):
+                msum[t, j * (STEP // 4) + i // 4, i % 4] = out[:, i * B : (i + 1) * B]
             return 0
 
-        lax.fori_loop(0, 8, mirror_near, 0)
+        lax.fori_loop(0, 16 // STEP, mirror_near, 0)
         own_y = jnp.concatenate([vcol[t, y * NL + i] for i in range(NL)], axis=1)
 
         def direct_near(j, _):
-            rows = pl.ds(pl.multiple_of(j * pair, pair), pair)
+            rows = pl.ds(pl.multiple_of(j * wide, wide), wide)
             out = lax.dot_general(
                 own_y,
                 matrix[rows, pl.ds(pl.multiple_of(y * quarter, quarter), quarter)],
                 (((1,), (1,)), ((), ())),
                 preferred_element_type=F32,
             )
-            dsum[t, 0, j % 4, j // 4] = out[:, :B]
-            dsum[t, 1, j % 4, j // 4] = out[:, B:]
+            for i in range(STEP):
+                b = j * STEP + i
+                dsum[t, i % 2, b // 2 % 4, b // 8] = out[:, i * B : (i + 1) * B]
             return 0
 
-        lax.fori_loop(0, 8, direct_near, 0)
+        lax.fori_loop(0, 16 // STEP, direct_near, 0)
         if t > 0:
             gram_cps = gram_z(t, gram_cps)
         wait_all(cps_y)
-        others = []
-        for d in range(1, NY):
-            yy = (y + d) % NY
-            others.append(
-                (yy, jnp.concatenate([vcol[t, yy * NL + i] for i in range(NL)], axis=1))
+        around = [(y + d) % NY for d in range(1, NY)]
+        others = jnp.concatenate(
+            [vcol[t, yy * NL + i] for yy in around for i in range(NL)], axis=1
+        )
+
+        def direct_far(parity):
+            stored = jnp.concatenate(
+                [
+                    jnp.concatenate(
+                        [
+                            matrix[
+                                pl.ds(pl.multiple_of((2 * i + parity) * B, B), B),
+                                pl.ds(pl.multiple_of(yy * quarter, quarter), quarter),
+                            ]
+                            for yy in around
+                        ],
+                        axis=1,
+                    )
+                    for i in range(8)
+                ],
+                axis=0,
             )
-
-        def direct_far(j, _):
-            rows = pl.ds(pl.multiple_of(j * pair, pair), pair)
-            out = 0.0
-            for yy, values in others:
-                out = out + lax.dot_general(
-                    values,
-                    matrix[rows, pl.ds(pl.multiple_of(yy * quarter, quarter), quarter)],
-                    (((1,), (1,)), ((), ())),
-                    preferred_element_type=F32,
-                )
-            dsum[t, 0, j % 4, j // 4] += out[:, :B]
-            dsum[t, 1, j % 4, j // 4] += out[:, B:]
-            return 0
-
-        lax.fori_loop(0, 8, direct_far, 0)
+            out = lax.dot_general(
+                others, stored, (((1,), (1,)), ((), ())), preferred_element_type=F32
+            )
+            for i in range(8):
+                dsum[t, parity, i % 4, i // 4] += out[:, i * B : (i + 1) * B]
+
+        direct_far(1 - core)
         cps_c = rs_core(dsum.at[t], rc.at[t])
         wait_all(cps_far)
         far = jnp.concatenate([vrow[t, (1 - h) * rest + i] for i in range(rest)], axis=1)
 
         def mirror_far(j, _):
-            cols = pl.ds(pl.multiple_of(j * pair, pair), pair)
+            cols = pl.ds(pl.multiple_of(j * wide, wide), wide)
             out = jnp.dot(
                 far,
                 matrix[pl.ds(pl.multiple_of((1 - h) * half, half), half), cols],
                 preferred_element_type=F32,
             )
-            msum[t, j // 2, 2 * (j % 2)] += out[:, :B]
-            msum[t, j // 2, 2 * (j % 2) + 1] += out[:, B:]
+            for i in range(STEP):
+                msum[t, j * (STEP // 4) + i // 4, i % 4] += out[:, i * B : (i + 1) * B]
             return 0
 
-        lax.fori_loop(0, 8, mirror_far, 0)
+        lax.fori_loop(0, 16 // STEP, mirror_far, 0)
         cps_r = ring_start(msum.at[t], yq.at[t], y, device_y)
+        direct_far(core)
         wait_all(cps_c)
         d1[t] = dsum[t, core] + rc[t]
         cps_c = ring_start(d1.at[t], xq.at[t], x, device_x)

time: 137 us -> 126 us (0.920)
  Pallas kernels: 136 us -> 124 us
    pallas_call x1, Pallas kernels: 136 us -> 124 us  [local(): pl.pallas_call(kernel, out_shape=jax.ShapeDtypeStruct(blk, F32), in_specs...]
where the time goes in v3:
time: 126 us
  Pallas kernels  124 us (98%)
  other arithmetic  1.38 us (1%)
    pallas_call x1, Pallas kernels, local(): pl.pallas_call(kernel, out_shape=jax.ShapeDtypeStruct(blk, F32), in_specs...  124 us

profile of v3, /device:TPU:1, one launch (start us, length us, event | category | flops | bytes accessed | tf_op | source)
XLA Modules:
  0.0 125.6 jit_solution(6835085282911575111)
XLA Ops:
  0.0 124.2 %shard_map.46 = f32[64,128]{1,0:T(8,128)} custom-call(f32[64,128]{1,0:T(8,128)} %start_hbm.1, s32[1,128]{1,0:T(1,128)} %order_hbm.1, s32[16,1,16]{2,1,0:T(1,128)} %mask_hbm.1, bf16[2048,2048]{1,0:T(8,128)(2,1)} %bitcast.1), custom_call_target="tpu_custom_call" | custom-call | tf_op jit(solution)/shard_map/pallas_call | solution.py:574
  124.2 1.4 %broadcast_multiply_fusion = f32[64,128]{1,0:T(8,128)} fusion(f32[64,128]{1,0:T(8,128)} %shard_map.46), kind=kLoop, calls=%fused_computation | loop fusion | flops 8192 | bytes 65536 | tf_op jit(solution)/shard_map/mul | solution.py:584

commit v4 on v3

--- a/solution.py
+++ b/solution.py
@@ -13,6 +13,7 @@
 B = 128
 GROUP = 4
 STEP = 8
+FLIP = 256
 NY, NL, NH, NX, NC = 4, 4, 2, 4, 2
 MESH = pl.DeviceIdType.MESH
 HI = lax.Precision.HIGHEST
@@ -40,13 +41,23 @@
         columns = [column_of_all(block, 8 * b + m) for m in range(8)]
         pivots = {(k, m): row_of_all(columns[m], k) for m in range(8) for k in range(m, 8)}
         lower, inverses, reduced = {}, [], []
-        for m in range(8):
-            inverses.append(1.0 / pivots[m, m])
-            for k in range(m + 1, 8):
-                lower[k, m] = pivots[k, m] * inverses[m]
-            for k in range(m + 1, 8):
-                for n in range(m + 1, k + 1):
-                    pivots[k, n] = pivots[k, n] - lower[k, m] * pivots[n, m]
+        for m in range(0, 8, 2):
+            n = m + 1
+            first, cross, second = pivots[m, m], pivots[n, m], pivots[n, n]
+            one = 1.0 / first
+            two = first * (1.0 / (first * second - cross * cross))
+            inverses += [one, two]
+            lower[n, m] = cross * one
+            pivots[n, n] = second - cross * lower[n, m]
+            for k in range(m + 2, 8):
+                lower[k, m] = pivots[k, m] * one
+                pivots[k, n] = pivots[k, n] - pivots[k, m] * lower[n, m]
+                lower[k, n] = pivots[k, n] * two
+            for k in range(m + 2, 8):
+                for i in range(m + 2, k + 1):
+                    pivots[k, i] = (pivots[k, i] - lower[k, m] * pivots[i, m]) - lower[
+                        k, n
+                    ] * pivots[i, n]
         for k in range(8):
             value = row_of_all(block, k)
             for m in range(k):
@@ -81,6 +92,7 @@
     order_ref,
     mask_ref,
     matrix,
+    flipped,
     wdiag,
     vsend,
     vrow,
@@ -253,37 +265,30 @@
             out.append(send(mid.at[ll], dst.at[d - 1], row_of(y, ll), c))
         return out
 
-    first, second = pl.ds(0, K // 2), pl.ds(K // 2, K // 2)
-
-    def ring_start(src, q, p, device):
-        ahead, behind, across = (p + 1) % 4, (p + 3) % 4, (p + 2) % 4
+    def ring_start(src, short, q, p, device):
+        short[...] = src[...].astype(BF)
         return [
-            send(src.at[across, :, first, :], q.at[0], *device(ahead)),
-            send(src.at[across, :, second, :], q.at[1], *device(behind)),
-            send(src.at[ahead, :, second, :], q.at[2], *device(ahead)),
-            send(src.at[behind, :, first, :], q.at[3], *device(behind)),
-        ]
-
-    def ring_mid(cps, src, q, mid, p, device):
-        ahead, behind = (p + 1) % 4, (p + 3) % 4
-        cps[0].wait_recv()
-        mid[0] = src[ahead, :, first, :] + q[0]
-        forth = send(mid.at[0], q.at[4], *device(ahead))
-        cps[1].wait_recv()
-        mid[1] = src[behind, :, second, :] + q[1]
-        back = send(mid.at[1], q.at[5], *device(behind))
-        return cps[2:] + [forth, back]
+            send(short.at[(p + d) % 4], q.at[d - 1], *device((p + d) % 4)) for d in (2, 1, 3)
+        ]
 
     def ring_end(cps, src, q, p, dst):
         wait_all(cps)
-        dst[:, first, :] = (src[p, :, first, :] + q[3]) + q[4]
-        dst[:, second, :] = (src[p, :, second, :] + q[2]) + q[5]
+        dst[...] = (src[p] + q[0].astype(F32)) + (q[1].astype(F32) + q[2].astype(F32))
 
     def device_x(p):
         return r, col_of(h, p * NC + core)
 
     def device_y(p):
         return row_of(p, l), c
+
+    def flip(part):
+        def step(j, _):
+            rows = pl.ds(pl.multiple_of(j * FLIP, FLIP), FLIP)
+            flipped[:, rows] = matrix[rows, :].T
+            return 0
+
+        count = 16 * B // FLIP // 2
+        lax.fori_loop(part * count, (part + 1) * count, step, 0)
 
     local_copies[0].wait()
     local_copies[1].wait()
@@ -353,10 +358,12 @@
     cps_c = [
         send(ed1.at[(x + d) % NX], erx.at[d - 1], *device_x((x + d) % NX)) for d in range(1, NX)
     ]
+    flip(0)
     wait_all(cps_r)
     em1[...] = ((emsum[y] + ery[0]) + ery[1]) + ery[2]
     cps_r = rs_l(em1, erl)
     gram_cps = gram_z(0, gram_cps)
+    flip(1)
     wait_all(cps_c)
     ed2[...] = ((ed1[x] + erx[0]) + erx[1]) + erx[2]
     cps_c = rs_h(ed2, erz)
@@ -369,7 +376,6 @@
     panel = jnp.dot(factor, panel, precision=HI, preferred_element_type=F32)
 
     half = 8 * B
-    quarter = 4 * B
     wide = STEP * B
 
     for t in range(ITERS):
@@ -417,14 +423,23 @@
             return 0
 
         lax.fori_loop(0, 16 // STEP, mirror_near, 0)
-        own_y = jnp.concatenate([vcol[t, y * NL + i] for i in range(NL)], axis=1)
+        wait_all(cps_y[: NY - 1])
+        around = [(y + d) % NY for d in range(1, NY)]
+        early = jnp.concatenate(
+            [vcol[t, y * NL + i] for i in range(NL)] + [vcol[t, row_of(yy, l)] for yy in around],
+            axis=1,
+        )
+
+        def stored_rows(blocks, cols):
+            return jnp.concatenate(
+                [flipped[pl.ds(pl.multiple_of(i * B, B), B), cols] for i in blocks], axis=0
+            )
 
         def direct_near(j, _):
-            rows = pl.ds(pl.multiple_of(j * wide, wide), wide)
-            out = lax.dot_general(
-                own_y,
-                matrix[rows, pl.ds(pl.multiple_of(y * quarter, quarter), quarter)],
-                (((1,), (1,)), ((), ())),
+            cols = pl.ds(pl.multiple_of(j * wide, wide), wide)
+            out = jnp.dot(
+                early,
+                stored_rows([y * NL + i for i in range(NL)] + [row_of(yy, l) for yy in around], cols),
                 preferred_element_type=F32,
             )
             for i in range(STEP):
@@ -433,34 +448,34 @@
             return 0
 
         lax.fori_loop(0, 16 // STEP, direct_near, 0)
-        if t > 0:
-            gram_cps = gram_z(t, gram_cps)
-        wait_all(cps_y)
-        around = [(y + d) % NY for d in range(1, NY)]
-        others = jnp.concatenate(
-            [vcol[t, yy * NL + i] for yy in around for i in range(NL)], axis=1
-        )
+        def forwarded(d):
+            return [row_of(yy, (l + NL - d) % NL) for yy in around]
+
+        wait_all(cps_y[NY - 1 : 2 * (NY - 1)])
+        middle = jnp.concatenate([vcol[t, i] for i in forwarded(1)], axis=1)
+
+        def direct_middle(j, _):
+            cols = pl.ds(pl.multiple_of(j * wide, wide), wide)
+            out = jnp.dot(middle, stored_rows(forwarded(1), cols), preferred_element_type=F32)
+            for i in range(STEP):
+                b = j * STEP + i
+                dsum[t, i % 2, b // 2 % 4, b // 8] += out[:, i * B : (i + 1) * B]
+            return 0
+
+        lax.fori_loop(0, 16 // STEP, direct_middle, 0)
+        wait_all(cps_y[2 * (NY - 1) :])
+        late = forwarded(2) + forwarded(3)
+        others = jnp.concatenate([vcol[t, i] for i in late], axis=1)
 
         def direct_far(parity):
             stored = jnp.concatenate(
                 [
-                    jnp.concatenate(
-                        [
-                            matrix[
-                                pl.ds(pl.multiple_of((2 * i + parity) * B, B), B),
-                                pl.ds(pl.multiple_of(yy * quarter, quarter), quarter),
-                            ]
-                            for yy in around
-                        ],
-                        axis=1,
-                    )
+                    stored_rows(late, pl.ds(pl.multiple_of((2 * i + parity) * B, B), B))
                     for i in range(8)
                 ],
-                axis=0,
+                axis=1,
             )
-            out = lax.dot_general(
-                others, stored, (((1,), (1,)), ((), ())), preferred_element_type=F32
-            )
+            out = jnp.dot(others, stored, preferred_element_type=F32)
             for i in range(8):
                 dsum[t, parity, i % 4, i // 4] += out[:, i * B : (i + 1) * B]
 
@@ -481,19 +496,19 @@
             return 0
 
         lax.fori_loop(0, 16 // STEP, mirror_far, 0)
-        cps_r = ring_start(msum.at[t], yq.at[t], y, device_y)
+        cps_r = ring_start(msum.at[t], ym.at[t], yq.at[t], y, device_y)
+        if t > 0:
+            gram_cps = gram_z(t, gram_cps)
         direct_far(core)
         wait_all(cps_c)
         d1[t] = dsum[t, core] + rc[t]
-        cps_c = ring_start(d1.at[t], xq.at[t], x, device_x)
-        if t > 0:
-            gram_cps = gram_all(t, gram_cps)
-        cps_c = ring_mid(cps_c, d1.at[t], xq.at[t], xm.at[t], x, device_x)
-        cps_r = ring_mid(cps_r, msum.at[t], yq.at[t], ym.at[t], y, device_y)
+        cps_c = ring_start(d1.at[t], xm.at[t], xq.at[t], x, device_x)
         ring_end(cps_c, d1.at[t], xq.at[t], x, d2.at[t])
         cps_c = rs_h(d2.at[t], rz.at[t])
         ring_end(cps_r, msum.at[t], yq.at[t], y, m1.at[t])
         cps_r = rs_l(m1.at[t], rl.at[t])
+        if t > 0:
+            gram_cps = gram_all(t, gram_cps)
         if t > 0:
             factor = gram_end(t, gram_cps)
         wait_all(cps_r)
@@ -505,6 +520,10 @@
 
     gram_local(ITERS, panel)
     gram_cps = gram_start(ITERS)
+    done = len(pending)
+    for cp in pending[: done - 7]:
+        cp.wait_send()
+    del pending[: done - 7]
     gram_cps = gram_y(ITERS, gram_cps)
     gram_cps = gram_z(ITERS, gram_cps)
     gram_cps = gram_all(ITERS, gram_cps)
@@ -517,7 +536,7 @@
 def copies():
     gram = 7 + 3 + 7 + 7
     degrees = 1 + 3 + 1 + 3 + 3
-    scatter = 1 + 6 + 1 + 6 + 3
+    scatter = 1 + 3 + 1 + 3 + 3
     gather = 1 + 3 + 7 + 3 + 9 + 7
     return (ITERS + 1) * gram + degrees + ITERS * (scatter + gather)
 
@@ -526,12 +545,12 @@
     vm = pltpu.VMEM
     n = ITERS
     blk = (K, B)
-    hblk = (K // 2, B)
     eblk = (8, B)
     scratch = [
         vm(blk, F32),
         vm((1, B), jnp.int32),
         vm((16, 1, 16), jnp.int32),
+        vm((16 * B, 16 * B), BF),
         vm((16 * B, 16 * B), BF),
         vm((B, B), BF),
         vm((n,) + blk, BF),
@@ -541,13 +560,13 @@
         vm((n, NX, NH) + blk, F32),
         vm((n, NH) + blk, F32),
         vm((n, NX, NH) + blk, F32),
-        vm((n, 6, NH) + hblk, F32),
-        vm((n, 2, NH) + hblk, F32),
+        vm((n, NX - 1, NH) + blk, BF),
+        vm((n, NX, NH) + blk, BF),
         vm((n,) + blk, F32),
         vm((n, NY, NL) + blk, F32),
         vm((n, NL) + blk, F32),
-        vm((n, 6, NL) + hblk, F32),
-        vm((n, 2, NL) + hblk, F32),
+        vm((n, NY - 1, NL) + blk, BF),
+        vm((n, NY, NL) + blk, BF),
         vm((n, NL - 1) + blk, F32),
         vm((NC, NX, NH) + eblk, F32),
         vm((NX, NH) + eblk, F32),
@@ -578,9 +597,14 @@
         out_specs=pl.BlockSpec(memory_space=pltpu.VMEM),
         scratch_shapes=scratch,
         compiler_params=pltpu.CompilerParams(
-            collective_id=0, has_side_effects=True, vmem_limit_bytes=66 * 1000 * 1000
+            collective_id=0, has_side_effects=True, vmem_limit_bytes=50 * 1000 * 1000
         ),
-    )(start_vectors, cluster_order, block_mask, weights[:, 0, :])
+    )(
+        *[
+            pltpu.with_memory_space_constraint(v, pltpu.HBM)
+            for v in (start_vectors, cluster_order, block_mask, weights[:, 0, :])
+        ]
+    )
     return math.sqrt(16 * 16 * B) * panel
 
 

time: 126 us -> 113 us (0.90)
  Pallas kernels: 124 us -> 113 us
    pallas_call x1, Pallas kernels: 124 us -> 113 us  [local(): pl.pallas_call(kernel, out_shape=jax.ShapeDtypeStruct(blk, F32), in_specs...]
where the time goes in v4:
time: 113 us
  Pallas kernels  113 us (100%)
    pallas_call x1, Pallas kernels, local(): pl.pallas_call(kernel, out_shape=jax.ShapeDtypeStruct(blk, F32), in_specs...  113 us

profile of v4, /device:TPU:1, one launch (start us, length us, event | category | flops | bytes accessed | tf_op | source)
XLA Modules:
  0.0 113.3 jit_solution(16749972283828170947)
XLA Ops:
  0.0 112.6 %shard_map.46 = f32[64,128]{1,0:T(8,128)S(1)} custom-call(f32[64,128]{1,0:T(8,128)} %start_hbm.1, s32[1,128]{1,0:T(1,128)} %order_hbm.1, s32[16,1,16]{2,1,0:T(1,128)} %mask_hbm.1, bf16[2048,2048]{1,0:T(8,128)(2,1)} %bitcast.1), custom_call_target="tpu_custom_call" | custom-call | tf_op jit(solution)/shard_map/pallas_call | solution.py:593
  112.6 0.6 broadcast_multiply_fusion

commit v5 on v4

--- a/solution.py
+++ b/solution.py
@@ -100,12 +100,14 @@
     dsum,
     d1,
     d2,
+    d3,
     rc,
     xq,
     xm,
     rz,
     msum,
     m1,
+    m2,
     yq,
     ym,
     rl,
@@ -219,31 +221,31 @@
             for d in range(1, rest)
         ]
 
-    def gram_y(t, cps):
+    def gram_z(t, cps):
         wait_all(cps)
         total = gs[t, e]
         for d in range(rest - 1):
             total = total + ga[t, d]
         g1[t] = total
-        return [
-            send(g1.at[t], gy.at[t, d - 1], row_of((y + d) % NY, l), c) for d in range(1, NY)
-        ]
-
-    def gram_z(t, cps):
-        wait_all(cps)
-        g2[t] = ((g1[t] + gy[t, 0]) + gy[t, 1]) + gy[t, 2]
         out = []
         for d in range(1, NH * NL):
             zz = (z + d) % (NH * NL)
-            out.append(send(g2.at[t], gz.at[t, d - 1], row_of(y, zz % NL), col_of(zz // NL, e)))
+            out.append(send(g1.at[t], gz.at[t, d - 1], row_of(y, zz % NL), col_of(zz // NL, e)))
         return out
+
+    def gram_y(t, cps):
+        wait_all(cps)
+        total = g1[t]
+        for d in range(NH * NL - 1):
+            total = total + gz[t, d]
+        g2[t] = total
+        return [
+            send(g2.at[t], gy.at[t, d - 1], row_of((y + d) % NY, l), c) for d in range(1, NY)
+        ]
 
     def gram_all(t, cps):
         wait_all(cps)
-        total = g2[t]
-        for d in range(NH * NL - 1):
-            total = total + gz[t, d]
-        gf[t, e] = total
+        gf[t, e] = ((g2[t] + gy[t, 0]) + gy[t, 1]) + gy[t, 2]
         return [
             send(gf.at[t, e], gf.at[t, e], r, col_of(h, (e + d) % rest)) for d in range(1, rest)
         ]
@@ -352,7 +354,7 @@
         send(emsum.at[(y + d) % NY], ery.at[d - 1], row_of((y + d) % NY, l), c)
         for d in range(1, NY)
     ]
-    gram_cps = gram_y(0, gram_cps)
+    gram_cps = gram_z(0, gram_cps)
     wait_all(cps_c)
     ed1[...] = edsum[core] + erc[...]
     cps_c = [
@@ -362,7 +364,7 @@
     wait_all(cps_r)
     em1[...] = ((emsum[y] + ery[0]) + ery[1]) + ery[2]
     cps_r = rs_l(em1, erl)
-    gram_cps = gram_z(0, gram_cps)
+    gram_cps = gram_y(0, gram_cps)
     flip(1)
     wait_all(cps_c)
     ed2[...] = ((ed1[x] + erx[0]) + erx[1]) + erx[2]
@@ -388,15 +390,15 @@
         cps_l = [
             send(own, vcol.at[t, r], row_of(y, (l + d) % NL), c) for d in range(1, NL)
         ]
-        cps_e = [
-            send(own, vrow.at[t, c], r, col_of(h, (e + d) % rest)) for d in range(1, rest)
-        ]
         cps_y = [
             send(own, vcol.at[t, r], row_of((y + d) % NY, l), c) for d in range(1, NY)
         ]
         if t > 0:
             gram_local(t, panel)
             gram_cps = gram_start(t)
+        cps_e = [
+            send(own, vrow.at[t, c], r, col_of(h, (e + d) % rest)) for d in range(1, rest)
+        ]
         for d in range(1, NL):
             cps_l[d - 1].wait_recv()
             got = vcol.at[t, row_of(y, (l - d + NL) % NL)]
@@ -406,7 +408,7 @@
         got = vrow.at[t, col_of(1 - h, e)]
         cps_far = [send(got, got, r, col_of(h, (e + d) % rest)) for d in range(1, rest)]
         if t > 0:
-            gram_cps = gram_y(t, gram_cps)
+            gram_cps = gram_z(t, gram_cps)
 
         wait_all(cps_e)
         near = jnp.concatenate([vrow[t, h * rest + i] for i in range(rest)], axis=1)
@@ -481,6 +483,8 @@
 
         direct_far(1 - core)
         cps_c = rs_core(dsum.at[t], rc.at[t])
+        if t > 0:
+            gram_cps = gram_y(t, gram_cps)
         wait_all(cps_far)
         far = jnp.concatenate([vrow[t, (1 - h) * rest + i] for i in range(rest)], axis=1)
 
@@ -497,23 +501,25 @@
 
         lax.fori_loop(0, 16 // STEP, mirror_far, 0)
         cps_r = ring_start(msum.at[t], ym.at[t], yq.at[t], y, device_y)
-        if t > 0:
-            gram_cps = gram_z(t, gram_cps)
         direct_far(core)
         wait_all(cps_c)
         d1[t] = dsum[t, core] + rc[t]
         cps_c = ring_start(d1.at[t], xm.at[t], xq.at[t], x, device_x)
-        ring_end(cps_c, d1.at[t], xq.at[t], x, d2.at[t])
-        cps_c = rs_h(d2.at[t], rz.at[t])
-        ring_end(cps_r, msum.at[t], yq.at[t], y, m1.at[t])
-        cps_r = rs_l(m1.at[t], rl.at[t])
         if t > 0:
             gram_cps = gram_all(t, gram_cps)
+        ring_end(cps_c, d1.at[t], xq.at[t], x, d2.at[t])
+        d3[t] = d2[t, 1 - h].astype(BF)
+        cps_c = [send(d3.at[t], rz.at[t], r, col_of(1 - h, e))]
+        ring_end(cps_r, msum.at[t], yq.at[t], y, m1.at[t])
+        m2[t] = m1[t].astype(BF)
+        cps_r = rs_l(m2.at[t], rl.at[t])
         if t > 0:
             factor = gram_end(t, gram_cps)
         wait_all(cps_r)
         wait_all(cps_c)
-        product = (d2[t, h] + rz[t]) + (((m1[t, l] + rl[t, 0]) + rl[t, 1]) + rl[t, 2])
+        product = (d2[t, h] + rz[t].astype(F32)) + (
+            ((m1[t, l] + rl[t, 0].astype(F32)) + rl[t, 1].astype(F32)) + rl[t, 2].astype(F32)
+        )
         panel = panel + inverse_root * product
         if t > 0:
             panel = jnp.dot(factor, panel, precision=HI, preferred_element_type=F32)
@@ -524,8 +530,8 @@
     for cp in pending[: done - 7]:
         cp.wait_send()
     del pending[: done - 7]
+    gram_cps = gram_z(ITERS, gram_cps)
     gram_cps = gram_y(ITERS, gram_cps)
-    gram_cps = gram_z(ITERS, gram_cps)
     gram_cps = gram_all(ITERS, gram_cps)
     factor = gram_end(ITERS, gram_cps)
     out_ref[...] = jnp.dot(factor, panel, precision=HI, preferred_element_type=F32)
@@ -559,15 +565,17 @@
         vm((n, NC, NX, NH) + blk, F32),
         vm((n, NX, NH) + blk, F32),
         vm((n, NH) + blk, F32),
+        vm((n,) + blk, BF),
         vm((n, NX, NH) + blk, F32),
         vm((n, NX - 1, NH) + blk, BF),
         vm((n, NX, NH) + blk, BF),
-        vm((n,) + blk, F32),
+        vm((n,) + blk, BF),
         vm((n, NY, NL) + blk, F32),
         vm((n, NL) + blk, F32),
+        vm((n, NL) + blk, BF),
         vm((n, NY - 1, NL) + blk, BF),
         vm((n, NY, NL) + blk, BF),
-        vm((n, NL - 1) + blk, F32),
+        vm((n, NL - 1) + blk, BF),
         vm((NC, NX, NH) + eblk, F32),
         vm((NX, NH) + eblk, F32),
         vm((NH,) + eblk, F32),

time: 113 us -> 110 us (0.973)
  Pallas kernels: 113 us -> 109 us
    pallas_call x1, Pallas kernels: 113 us -> 109 us  [local(): pl.pallas_call(kernel, out_shape=jax.ShapeDtypeStruct(blk, F32), in_specs...]
where the time goes in v5:
time: 110 us
  Pallas kernels  109 us (99%)
    pallas_call x1, Pallas kernels, local(): pl.pallas_call(kernel, out_shape=jax.ShapeDtypeStruct(blk, F32), in_specs...  109 us

profile of v5, /device:TPU:1, one launch (start us, length us, event | category | flops | bytes accessed | tf_op | source)
XLA Modules:
  0.0 109.5 jit_solution(5456936852183287203)
XLA Ops:
  0.0 108.9 %shard_map.46 = f32[64,128]{1,0:T(8,128)S(1)} custom-call(f32[64,128]{1,0:T(8,128)} %start_hbm.1, s32[1,128]{1,0:T(1,128)} %order_hbm.1, s32[16,1,16]{2,1,0:T(1,128)} %mask_hbm.1, bf16[2048,2048]{1,0:T(8,128)(2,1)} %bitcast.1), custom_call_target="tpu_custom_call" | custom-call | tf_op jit(solution)/shard_map/pallas_call | solution.py:601
  108.9 0.6 broadcast_multiply_fusion

commit v6 on v5

--- a/solution.py
+++ b/solution.py
@@ -124,7 +124,6 @@
     gs,
     ga,
     g1,
-    gy,
     g2,
     gz,
     gf,
@@ -146,6 +145,9 @@
     def row_of(yy, ll):
         return yy * NL + ll
 
+    def device_ye(d):
+        return row_of((y + d // rest) % NY, l), col_of(h, (e + d) % rest)
+
     barrier = pltpu.get_barrier_semaphore()
     for d in range(1, NH * NL):
         zz = (z + d) % (NH * NL)
@@ -155,13 +157,9 @@
             device_id=(row_of(y, zz % NL), col_of(zz // NL, e)),
             device_id_type=MESH,
         )
-    for d in range(1, NY):
+    for d in range(1, NY * rest):
         pl.semaphore_signal(
-            barrier, inc=1, device_id=(row_of((y + d) % NY, l), c), device_id_type=MESH
-        )
-    for d in range(1, rest):
-        pl.semaphore_signal(
-            barrier, inc=1, device_id=(r, col_of(h, (e + d) % rest)), device_id_type=MESH
+            barrier, inc=1, device_id=device_ye(d), device_id_type=MESH
         )
 
     local_copies = []
@@ -208,12 +206,13 @@
             cp.wait_recv()
 
     def gram_local(t, panel):
-        padded = jnp.concatenate([jnp.zeros((K, B), F32), panel], axis=0)
         gram = lax.dot_general(
-            panel, padded, (((1,), (1,)), ((), ())), precision=HI, preferred_element_type=F32
+            panel, panel, (((1,), (1,)), ((), ())), precision=HI, preferred_element_type=F32
         )
         for g in range(8):
-            gs[t, g] = gram[8 * g : 8 * g + 8]
+            gs[t, g] = jnp.concatenate(
+                [gram[8 * g : 8 * g + 4], gram[8 * g + 4 : 8 * g + 8]], axis=1
+            )
 
     def gram_start(t):
         return [
@@ -233,26 +232,26 @@
             out.append(send(g1.at[t], gz.at[t, d - 1], row_of(y, zz % NL), col_of(zz // NL, e)))
         return out
 
-    def gram_y(t, cps):
+    def gram_all(t, cps):
         wait_all(cps)
         total = g1[t]
         for d in range(NH * NL - 1):
             total = total + gz[t, d]
         g2[t] = total
+        gf[t, y, e] = total
         return [
-            send(g2.at[t], gy.at[t, d - 1], row_of((y + d) % NY, l), c) for d in range(1, NY)
-        ]
-
-    def gram_all(t, cps):
-        wait_all(cps)
-        gf[t, e] = ((g2[t] + gy[t, 0]) + gy[t, 1]) + gy[t, 2]
-        return [
-            send(gf.at[t, e], gf.at[t, e], r, col_of(h, (e + d) % rest)) for d in range(1, rest)
+            send(g2.at[t], gf.at[t, y, e], *device_ye(d)) for d in range(1, NY * rest)
         ]
 
     def gram_end(t, cps):
         wait_all(cps)
-        return inverse_factor([gf[t, g] for g in range(8)])
+        blocks = []
+        for g in range(8):
+            half_block = (gf[t, 0, g] + gf[t, 1, g]) + (gf[t, 2, g] + gf[t, 3, g])
+            blocks.append(
+                jnp.concatenate([pltpu.roll(half_block, K, 1), half_block], axis=0)
+            )
+        return inverse_factor(blocks)
 
     def rs_core(src, dst):
         return [send(src.at[1 - core], dst, r, col_of(h, x * NC + 1 - core))]
@@ -337,7 +336,7 @@
         for i in range(group):
             edsum[(a + i) % 2, (a + i) // 2 % 4, (a + i) // 8] = totals[:, i * B : (i + 1) * B]
         if a == 0:
-            pl.semaphore_wait(barrier, NH * NL - 1 + NY - 1 + rest - 1)
+            pl.semaphore_wait(barrier, NH * NL - 1 + NY * rest - 1)
             gram_cps = gram_start(0)
     for i in range(16):
         emsum[i // NL, i % NL] = col_totals[:, i * B : (i + 1) * B]
@@ -364,12 +363,11 @@
     wait_all(cps_r)
     em1[...] = ((emsum[y] + ery[0]) + ery[1]) + ery[2]
     cps_r = rs_l(em1, erl)
-    gram_cps = gram_y(0, gram_cps)
+    gram_cps = gram_all(0, gram_cps)
     flip(1)
     wait_all(cps_c)
     ed2[...] = ((ed1[x] + erx[0]) + erx[1]) + erx[2]
     cps_c = rs_h(ed2, erz)
-    gram_cps = gram_all(0, gram_cps)
     wait_all(cps_r)
     wait_all(cps_c)
     degree = (ed2[h] + erz[...]) + (((em1[l] + erl[0]) + erl[1]) + erl[2]) + diag_degree
@@ -483,8 +481,6 @@
 
         direct_far(1 - core)
         cps_c = rs_core(dsum.at[t], rc.at[t])
-        if t > 0:
-            gram_cps = gram_y(t, gram_cps)
         wait_all(cps_far)
         far = jnp.concatenate([vrow[t, (1 - h) * rest + i] for i in range(rest)], axis=1)
 
@@ -531,7 +527,6 @@
         cp.wait_send()
     del pending[: done - 7]
     gram_cps = gram_z(ITERS, gram_cps)
-    gram_cps = gram_y(ITERS, gram_cps)
     gram_cps = gram_all(ITERS, gram_cps)
     factor = gram_end(ITERS, gram_cps)
     out_ref[...] = jnp.dot(factor, panel, precision=HI, preferred_element_type=F32)
@@ -540,7 +535,7 @@
 
 
 def copies():
-    gram = 7 + 3 + 7 + 7
+    gram = 7 + 7 + 31
     degrees = 1 + 3 + 1 + 3 + 3
     scatter = 1 + 3 + 1 + 3 + 3
     gather = 1 + 3 + 7 + 3 + 9 + 7
@@ -552,6 +547,7 @@
     n = ITERS
     blk = (K, B)
     eblk = (8, B)
+    gblk = (4, B)
     scratch = [
         vm(blk, F32),
         vm((1, B), jnp.int32),
@@ -586,13 +582,12 @@
         vm((NL,) + eblk, F32),
         vm((NY - 1, NL) + eblk, F32),
         vm((NL - 1,) + eblk, F32),
-        vm((n + 1, 8) + eblk, F32),
-        vm((n + 1, 7) + eblk, F32),
-        vm((n + 1,) + eblk, F32),
-        vm((n + 1, 3) + eblk, F32),
-        vm((n + 1,) + eblk, F32),
-        vm((n + 1, 7) + eblk, F32),
-        vm((n + 1, 8) + eblk, F32),
+        vm((n + 1, 8) + gblk, F32),
+        vm((n + 1, 7) + gblk, F32),
+        vm((n + 1,) + gblk, F32),
+        vm((n + 1,) + gblk, F32),
+        vm((n + 1, 7) + gblk, F32),
+        vm((n + 1, NY, 8) + gblk, F32),
         pltpu.SemaphoreType.DMA((20,)),
         pltpu.SemaphoreType.DMA((copies(),)),
         pltpu.SemaphoreType.DMA((copies(),)),

time: 110 us -> 109 us (level)
  no operation moved by 1% of the time
where the time goes in v6:
time: 109 us
  Pallas kernels  108 us (99%)
    pallas_call x1, Pallas kernels, local(): pl.pallas_call(kernel, out_shape=jax.ShapeDtypeStruct(blk, F32), in_specs...  108 us

profile of v6, /device:TPU:1, one launch (start us, length us, event | category | flops | bytes accessed | tf_op | source)
XLA Modules:
  0.0 108.5 jit_solution(9685848031420739079)
XLA Ops:
  0.0 107.9 %shard_map.46 = f32[64,128]{1,0:T(8,128)S(1)} custom-call(f32[64,128]{1,0:T(8,128)} %start_hbm.1, s32[1,128]{1,0:T(1,128)} %order_hbm.1, s32[16,1,16]{2,1,0:T(1,128)} %mask_hbm.1, bf16[2048,2048]{1,0:T(8,128)(2,1)} %bitcast.1), custom_call_target="tpu_custom_call" | custom-call | tf_op jit(solution)/shard_map/pallas_call | solution.py:596
  107.9 0.6 broadcast_multiply_fusion
